TPU v7x, 256 devices: a whole 4x4x8 slice. The times are simulated.
256 devices in a mesh: dp: 4 (over z_hi, core), expert: 64 (over x, y, z_lo).
Axes of the slice: x: 4, y: 4, z: 8 (z_hi: 2, z_lo: 4; z = z_hi * 4 + z_lo), core: 2. Of those that a mesh axis runs over, the one named last changes fastest.
Arguments:
- query: bfloat16 [2, 16384, 2560], P(None, ('dp', 'expert')), may hold values from -24 to 24
- keys: bfloat16 [2, 16384, 512], P(None, ('dp', 'expert')), may hold values from -4 to 4
- values: bfloat16 [2, 16384, 512], P(None, ('dp', 'expert')), may hold values from -6 to 6
- lengths: int32 [2, 256, 4], P(None, ('dp', 'expert')), may hold values from 0 to 64, as said below
- routes: int32 [2, 16384, 6], P(None, ('dp', 'expert')), may hold values from 0 to 63, as said below
- gates: float32 [2, 16384, 6], P(None, ('dp', 'expert')), may hold values from 0.05 to 0.4
- norm_gain: float32 [2560], replicated, may hold values from 0.1 to 1.9
- old_holds: int32 [64], replicated, may hold values from 0 to 63, as said below
- dup_experts: int32 [4], replicated, may hold values from 0 to 63, as said below
- w_gate: bfloat16 [64, 2560, 768], P('expert'), may hold values from -0.125 to 0.125
- w_up: bfloat16 [64, 2560, 768], P('expert'), may hold values from -0.125 to 0.125
- w_down: bfloat16 [64, 768, 2560], P('expert'), may hold values from -0.21875 to 0.21875
Outputs:
- layer_out: bfloat16 [2, 16384, 2560], P(None, ('dp', 'expert'))
Inputs may be any that keep to these rules, and one draw needn't show every extreme that they name: Each length is a multiple of 8; the 4 lengths of one device in one batch add up to 64. `routes`: each token names 6 different experts. `dup_experts`: 4 different experts. `old_holds`: each expert stands in exactly one slot.
All inputs are finite; a program needn't handle non-finite values.
Results may differ from a plain program's by a relative error of at most 0.0061.
Values may be sent and summed in bfloat16 or wider, within the bound.
A program may use at most 128 MiB of HBM per device.

v0:
```python
import jax
import jax.numpy as jnp
from jax import lax
from jax.sharding import PartitionSpec as P

HEAD_WIDTH = 128
CAP = 6


def attend(query, key_rows, value_rows, lengths):
    rows = query.shape[0]
    kv_heads = key_rows.shape[1] // HEAD_WIDTH
    query_group = query.shape[1] // HEAD_WIDTH // kv_heads
    ends = jnp.cumsum(lengths)
    position = lax.iota(jnp.int32, rows)
    request = jnp.sum((position[:, None] >= ends[None, :]).astype(jnp.int32), axis=1)
    allowed = (request[:, None] == request[None, :]) & (position[None, :] <= position[:, None])
    query_heads = query.reshape(rows, kv_heads, query_group, HEAD_WIDTH)
    key_heads = key_rows.reshape(rows, kv_heads, HEAD_WIDTH)
    value_heads = value_rows.reshape(rows, kv_heads, HEAD_WIDTH)
    router_logits = jnp.einsum(
        "qhgd,khd->hgqk", query_heads, key_heads, preferred_element_type=jnp.float32
    ) * HEAD_WIDTH ** (-0.5)
    router_logits = jnp.where(allowed[None, None], router_logits, -1e30)
    highest = jnp.max(router_logits, axis=-1, keepdims=True)
    weights = jnp.exp(router_logits - highest)
    probs = (weights / jnp.sum(weights, axis=-1, keepdims=True)).astype(jnp.bfloat16)
    mixed = jnp.einsum("hgqk,khd->qhgd", probs, value_heads, preferred_element_type=jnp.float32)
    return mixed.reshape(rows, kv_heads * query_group * HEAD_WIDTH)


def normalize(attn, gain):
    meansq = jnp.mean(attn * attn, axis=-1, keepdims=True)
    return (attn * lax.rsqrt(meansq + 1e-05) * gain).astype(jnp.bfloat16)


def expert_rows(rows, gate_mat, up_mat, down_mat):
    gate_val = jnp.dot(rows, gate_mat, preferred_element_type=jnp.float32)
    up_val = jnp.dot(rows, up_mat, preferred_element_type=jnp.float32)
    hidden = (jax.nn.silu(gate_val) * up_val).astype(jnp.bfloat16)
    return jnp.dot(hidden, down_mat, preferred_element_type=jnp.float32).astype(jnp.bfloat16)


def routing(routes, copies_of, first_target, second_target, regions):
    expert_list = lax.iota(jnp.int32, copies_of.shape[0])
    hit = (routes[:, :, None] == expert_list[None, None, :]).astype(jnp.int32)
    named = jnp.sum(hit, axis=1)
    before = jnp.cumsum(named, axis=0) - named
    place = jnp.sum(hit * before[:, None, :], axis=2)
    limit = jnp.sum(hit * copies_of[None, None, :], axis=2)
    kept = place < limit * CAP
    which = place // CAP
    target = jnp.where(
        which == 0,
        jnp.sum(hit * first_target[None, None, :], axis=2),
        jnp.sum(hit * second_target[None, None, :], axis=2),
    )
    flat = (target * CAP + place % CAP) * regions + which
    return (flat, kept)


def pack(normed, flat, kept, shape):
    slots = shape[0] * shape[1] * shape[2]
    spot = jnp.where(kept, flat, slots)
    hit = spot[None, :, :] == lax.iota(jnp.int32, slots)[:, None, None]
    picker = jnp.any(hit, axis=2).astype(normed.dtype).reshape(shape + (normed.shape[0],))
    packed = jnp.einsum("abct,tf->abcf", picker, normed, preferred_element_type=jnp.float32)
    return (packed.astype(normed.dtype), spot)


def gather_pack(normed, flat, kept, shape):
    slots = shape[0] * shape[1] * shape[2]
    tok_rows = normed.shape[0]
    token = jnp.broadcast_to(lax.iota(jnp.int32, tok_rows)[:, None], flat.shape)
    spot = jnp.where(kept, flat, slots)
    source_row = jnp.full((slots,), tok_rows, jnp.int32).at[spot].set(token, mode="drop")
    padded = jnp.concatenate([normed, jnp.zeros((1, normed.shape[1]), normed.dtype)], axis=0)
    return (padded[source_row].reshape(shape + (normed.shape[1],)), spot)


def combine(attn, returned, spot, kept, gates):
    slots = returned.size // returned.shape[-1]
    weight = jnp.where(kept, gates, 0.0)
    onehot = (spot[:, :, None] == lax.iota(jnp.int32, slots)[None, None, :]).astype(jnp.float32)
    spread = jnp.sum(onehot * weight[:, :, None], axis=1).reshape((-1,) + returned.shape[:-1])
    mixed = jnp.einsum(
        "tabc,abcf->tf",
        spread,
        returned.astype(jnp.float32),
        precision=lax.Precision.HIGHEST,
        preferred_element_type=jnp.float32,
    )
    return (attn + mixed).astype(jnp.bfloat16)


def shards(
    query,
    keys,
    values,
    lengths,
    routes,
    gates,
    norm_gain,
    old_holds,
    dup_experts,
    w_gate,
    w_up,
    w_down,
):
    width = lax.axis_size("expert")
    features = norm_gain.shape[0]
    expert_list = lax.iota(jnp.int32, old_holds.shape[0])
    holder = jnp.sum(
        expert_list[:, None] * (old_holds[:, None] == expert_list[None, :]).astype(jnp.int32),
        axis=0,
    )
    doubled = jnp.sum((dup_experts[:, None] == expert_list[None, :]).astype(jnp.int32), axis=0)
    own_gate, own_up, own_down = (w_gate[0], w_up[0], w_down[0])
    attn_one = attend(query[0], keys[0], values[0], lengths[0, 0])
    normed_one = normalize(attn_one, norm_gain)
    flat_one, kept_one = routing(routes[0], jnp.ones_like(doubled), holder, holder, 1)
    packed_one, spot_one = pack(normed_one, flat_one, kept_one, (width, CAP // 2, 2))
    received = lax.all_to_all(
        packed_one,
        "expert",
        split_axis=0,
        concat_axis=0,
        tiled=True,
    )
    result = expert_rows(received.reshape(-1, features), own_gate, own_up, own_down)
    back_one = lax.all_to_all(
        result.reshape(received.shape), "expert", split_axis=0, concat_axis=0, tiled=True
    )
    out_one = combine(attn_one, back_one, spot_one, kept_one, gates[0])
    attn_two = attend(query[1], keys[1], values[1], lengths[1, 0])
    normed_two = normalize(attn_two, norm_gain)
    flat_two, kept_two = routing(routes[1], 1 + doubled, holder, holder, 2)
    packed_two, spot_two = gather_pack(normed_two, flat_two, kept_two, (width, CAP, 2))
    received = lax.all_to_all(
        packed_two,
        "expert",
        split_axis=0,
        concat_axis=0,
        tiled=True,
    )
    result = expert_rows(received.reshape(-1, features), own_gate, own_up, own_down).reshape(
        received.shape
    )
    back_two = lax.all_to_all(result, "expert", split_axis=0, concat_axis=0, tiled=True)
    out_two = combine(attn_two, back_two, spot_two, kept_two, gates[1])
    return jnp.stack([out_one, out_two])


def solution(mesh):
    placed = (
        P(None, ("dp", "expert"), None),
        P(None, ("dp", "expert"), None),
        P(None, ("dp", "expert"), None),
        P(None, ("dp", "expert"), None),
        P(None, ("dp", "expert"), None),
        P(None, ("dp", "expert"), None),
        P(),
        P(),
        P(),
        P("expert", None, None),
        P("expert", None, None),
        P("expert", None, None),
    )
    return jax.shard_map(
        shards,
        mesh=mesh,
        in_specs=placed,
        out_specs=P(None, ("dp", "expert"), None),
        check_vma=False,
    )
```

profile of v0, /device:TPU:8, one launch (start us, length us, event | category | flops | bytes accessed | tf_op | source)
XLA Modules:
  0.0 319.2 jit_solution(5604583238541557621)
XLA Ops:
  7.8 3.3 %copy.95 = bf16[64,3,2,2560]{3,2,1,0:T(2,128)(2,1)} copy(bf16[64,3,2,2560]{3,0,2,1:T(8,128)(2,1)S(1)} %convolution_convert_fusion.2) | data formatting | bytes 3932160 | tf_op jit(solution)/shard_map/convert_element_type | solution.py:68
  11.1 12.0 %all-to-all-start = ((bf16[64,3,2,2560]{3,2,1,0:T(2,128)(2,1)}), bf16[64,3,2,2560]{3,2,1,0:T(2,128)(2,1)S(1)}, u32[]{:S(2)}, u32[]{:S(2)}) async-start(bf16[64,3,2,2560]{3,2,1,0:T(2,128)(2,1)} %copy.95), calls=%async_computation | async-start | bytes 3932160 | tf_op jit(solution)/shard_map/all_to_all | solution.py:123
  28.7 3.1 scatter_custom_fusion
  31.8 4.6 %gather_fusion = bf16[768,2560]{1,0:T(8,128)(2,1)} fusion(bf16[65,2560]{1,0:T(8,128)(2,1)S(1)} %concatenate.3, s32[1024]{0:T(1024)S(1)} %pad_clamp_fusion), kind=kCustom, calls=%fused_computation | custom fusion | bytes 7867392 | tf_op jit(solution)/shard_map/gather | solution.py:78
  36.4 8.7 %reshape.388 = bf16[64,6,2,2560]{3,2,1,0:T(2,128)(2,1)} reshape(bf16[768,2560]{1,0:T(8,128)(2,1)} %gather_fusion) | data formatting | bytes 7864320 | tf_op jit(solution)/shard_map/reshape | solution.py:78
  45.1 26.0 %all-to-all-done = bf16[64,3,2,2560]{3,2,1,0:T(2,128)(2,1)S(1)} async-done(((bf16[64,3,2,2560]{3,2,1,0:T(2,128)(2,1)}), bf16[64,3,2,2560]{3,2,1,0:T(2,128)(2,1)S(1)}, u32[]{:S(2)}, u32[]{:S(2)}) %all-to-all-start) | async-done | bytes 1966112 | tf_op jit(solution)/shard_map/all_to_all | solution.py:123
  71.1 6.4 %all-to-all-start.2 = ((bf16[64,6,2,2560]{3,2,1,0:T(2,128)(2,1)}), bf16[64,6,2,2560]{3,2,1,0:T(2,128)(2,1)}, u32[]{:S(2)}, u32[]{:S(2)}) async-start(bf16[64,6,2,2560]{3,2,1,0:T(2,128)(2,1)} %reshape.388), calls=%async_computation.2 | async-start | bytes 7864320 | tf_op jit(solution)/shard_map/all_to_all | solution.py:139
  77.6 2.3 reshape.382
  79.9 5.7 %fusion.10 = f32[384,768]{1,0:T(8,128)} fusion(bf16[384,2560]{1,0:T(8,128)(2,1)} %reshape.382, bf16[1,2560,768]{2,1,0:T(8,128)(2,1)} %param.21), kind=kOutput, calls=%fused_computation.15 | convolution fusion | flops 1509949440 | bytes 7077888 | tf_op jit(solution)/shard_map/dot_general | solution.py:38
  85.5 9.2 %convolution_convert_fusion.1 = bf16[384,2560]{1,0:T(8,128)(2,1)} fusion(bf16[1,768,2560]{2,1,0:T(8,128)(2,1)} %param.23, bf16[384,2560]{1,0:T(8,128)(2,1)S(1)} %copy-done.2, bf16[1,2560,768]{2,1,0:T(8,128)(2,1)} %param.22, f32[384,768]{1,0:T(8,128)} %fusion.10), kind=kOutput, calls=%fused_computation.5 | convolution fusion | flops 3022651392 | bytes 12976128 | tf_op jit(solution)/shard_map/dot_general | solution.py:41
  94.7 5.0 %reshape.383 = bf16[64,3,2,2560]{3,2,1,0:T(2,128)(2,1)} reshape(bf16[384,2560]{1,0:T(8,128)(2,1)} %convolution_convert_fusion.1) | data formatting | bytes 3932160 | tf_op jit(solution)/shard_map/reshape | solution.py:132
  99.7 66.6 %all-to-all-done.2 = bf16[64,6,2,2560]{3,2,1,0:T(2,128)(2,1)} async-done(((bf16[64,6,2,2560]{3,2,1,0:T(2,128)(2,1)}), bf16[64,6,2,2560]{3,2,1,0:T(2,128)(2,1)}, u32[]{:S(2)}, u32[]{:S(2)}) %all-to-all-start.2) | async-done | bytes 3932192 | tf_op jit(solution)/shard_map/all_to_all | solution.py:139
  166.3 5.7 %all-to-all-start.1 = ((bf16[64,3,2,2560]{3,2,1,0:T(2,128)(2,1)}), bf16[64,3,2,2560]{3,2,1,0:T(2,128)(2,1)S(1)}, u32[]{:S(2)}, u32[]{:S(2)}) async-start(bf16[64,3,2,2560]{3,2,1,0:T(2,128)(2,1)} %reshape.383), calls=%async_computation.1 | async-start | bytes 3932160 | tf_op jit(solution)/shard_map/all_to_all | solution.py:131
  172.0 9.1 %reshape.389 = bf16[768,2560]{1,0:T(8,128)(2,1)} reshape(bf16[64,6,2,2560]{3,2,1,0:T(2,128)(2,1)} %all-to-all-done.2) | data formatting | bytes 7864320 | tf_op jit(solution)/shard_map/reshape | solution.py:146
  181.1 6.6 %fusion.4 = f32[768,768]{1,0:T(8,128)S(1)} fusion(bf16[768,2560]{1,0:T(8,128)(2,1)} %reshape.389, bf16[1,2560,768]{2,1,0:T(8,128)(2,1)} %param.22), kind=kOutput, calls=%fused_computation.9 | convolution fusion | flops 3019898880 | bytes 10223616 | tf_op jit(solution)/shard_map/dot_general | solution.py:39
  187.8 3.4 %multiply_convert_fusion = bf16[768,768]{1,0:T(8,128)(2,1)S(1)} fusion(f32[768,768]{1,0:T(8,128)S(1)} %fusion.4, bf16[768,2560]{1,0:T(8,128)(2,1)S(1)} %copy-done, bf16[1,2560,768]{2,1,0:T(8,128)(2,1)S(1)} %copy-done.8), kind=kOutput, calls=%fused_computation.27 | convolution fusion | flops 3023437824 | bytes 11403264 | tf_op jit(solution)/shard_map/dot_general | solution.py:38
  191.2 4.8 %convolution_convert_fusion = bf16[768,2560]{1,0:T(8,128)(2,1)} fusion(bf16[768,768]{1,0:T(8,128)(2,1)S(1)} %multiply_convert_fusion, bf16[1,768,2560]{2,1,0:T(8,128)(2,1)S(1)} %copy-done.9), kind=kOutput, calls=%fused_computation.4 | convolution fusion | flops 3021864960 | bytes 9043968 | tf_op jit(solution)/shard_map/dot_general | solution.py:41
  196.0 8.7 %reshape.390 = bf16[64,6,2,2560]{3,2,1,0:T(2,128)(2,1)} reshape(bf16[768,2560]{1,0:T(8,128)(2,1)} %convolution_convert_fusion) | data formatting | bytes 7864320 | tf_op jit(solution)/shard_map/reshape | solution.py:146
  204.7 13.9 %all-to-all-done.1 = bf16[64,3,2,2560]{3,2,1,0:T(2,128)(2,1)S(1)} async-done(((bf16[64,3,2,2560]{3,2,1,0:T(2,128)(2,1)}), bf16[64,3,2,2560]{3,2,1,0:T(2,128)(2,1)S(1)}, u32[]{:S(2)}, u32[]{:S(2)}) %all-to-all-start.1) | async-done | bytes 1966112 | tf_op jit(solution)/shard_map/all_to_all | solution.py:131
  218.6 6.4 %all-to-all-start.3 = ((bf16[64,6,2,2560]{3,2,1,0:T(2,128)(2,1)}), bf16[64,6,2,2560]{3,2,1,0:T(2,128)(2,1)}, u32[]{:S(2)}, u32[]{:S(2)}) async-start(bf16[64,6,2,2560]{3,2,1,0:T(2,128)(2,1)} %reshape.390), calls=%async_computation.3 | async-start | bytes 7864320 | tf_op jit(solution)/shard_map/all_to_all | solution.py:149
  225.0 2.6 copy.88
  231.2 2.4 fusion.25
  233.6 80.2 %all-to-all-done.3 = bf16[64,6,2,2560]{3,2,1,0:T(2,128)(2,1)} async-done(((bf16[64,6,2,2560]{3,2,1,0:T(2,128)(2,1)}), bf16[64,6,2,2560]{3,2,1,0:T(2,128)(2,1)}, u32[]{:S(2)}, u32[]{:S(2)}) %all-to-all-start.3) | async-done | bytes 3932192 | tf_op jit(solution)/shard_map/all_to_all | solution.py:149
  313.8 4.5 %fusion.26 = bf16[1,64,2560]{2,1,0:T(8,128)(2,1)S(1)} fusion(f32[64,2560]{1,0:T(8,128)S(1)} %reshape.386, bf16[64,6,2,2560]{3,2,1,0:T(2,128)(2,1)} %all-to-all-done.3, f32[64,64,6,2]{0,3,2,1:T(2,128)S(1)} %bitcast.123), kind=kOutput, calls=%fused_computation.26 | convolution fusion | flops 1510277120 | bytes 5111808 | tf_op jit(solution)/shard_map/tabc,abcf->tf/dot_general | solution.py:86
  (90 shorter events, 17.5 us)
Async XLA Ops:
  0.0 2.5 copy-start.7
  0.0 3.8 %copy-start.5 = (s32[2,64,6]{1,0,2:T(2,128)S(1)}, s32[2,64,6]{1,0,2:T(2,128)}, u32[]{:S(2)}) copy-start(s32[2,64,6]{1,0,2:T(2,128)} %param.16) | copy-start | bytes 9220
  1.1 3.1 copy-start.10
  1.2 3.2 %copy-start.11 = (s32[64]{0:T(128)S(1)}, s32[64]{0:T(128)}, u32[]{:S(2)}) copy-start(s32[64]{0:T(128)} %param.19) | copy-start | bytes 772
  1.2 3.3 %copy-start.6 = (f32[2,64,6]{1,0,2:T(2,128)S(1)}, f32[2,64,6]{1,0,2:T(2,128)}, u32[]{:S(2)}) copy-start(f32[2,64,6]{1,0,2:T(2,128)} %param.17) | copy-start | bytes 9220
  1.2 4.6 %copy-start.3 = (bf16[2,64,512]{2,1,0:T(8,128)(2,1)S(1)}, bf16[2,64,512]{2,1,0:T(8,128)(2,1)}, u32[]{:S(2)}) copy-start(bf16[2,64,512]{2,1,0:T(8,128)(2,1)} %param.14) | copy-start | bytes 393220
  3.8 2.5 copy-start.4
  6.3 1.5 copy-start.1
  11.1 60.1 %all-to-all-start = ((bf16[64,3,2,2560]{3,2,1,0:T(2,128)(2,1)}), bf16[64,3,2,2560]{3,2,1,0:T(2,128)(2,1)S(1)}, u32[]{:S(2)}, u32[]{:S(2)}) async-start(bf16[64,3,2,2560]{3,2,1,0:T(2,128)(2,1)} %copy.95), calls=%async_computation | async-start | bytes 3932160 | tf_op jit(solution)/shard_map/all_to_all | solution.py:123
  71.1 95.2 %all-to-all-start.2 = ((bf16[64,6,2,2560]{3,2,1,0:T(2,128)(2,1)}), bf16[64,6,2,2560]{3,2,1,0:T(2,128)(2,1)}, u32[]{:S(2)}, u32[]{:S(2)}) async-start(bf16[64,6,2,2560]{3,2,1,0:T(2,128)(2,1)} %reshape.388), calls=%async_computation.2 | async-start | bytes 7864320 | tf_op jit(solution)/shard_map/all_to_all | solution.py:139
  79.9 5.7 %copy-start.2 = (bf16[384,2560]{1,0:T(8,128)(2,1)S(1)}, bf16[384,2560]{1,0:T(8,128)(2,1)}, u32[]{:S(2)}) copy-start(bf16[384,2560]{1,0:T(8,128)(2,1)} %reshape.382) | copy-start | bytes 5898244
  166.3 52.2 %all-to-all-start.1 = ((bf16[64,3,2,2560]{3,2,1,0:T(2,128)(2,1)}), bf16[64,3,2,2560]{3,2,1,0:T(2,128)(2,1)S(1)}, u32[]{:S(2)}, u32[]{:S(2)}) async-start(bf16[64,3,2,2560]{3,2,1,0:T(2,128)(2,1)} %reshape.383), calls=%async_computation.1 | async-start | bytes 3932160 | tf_op jit(solution)/shard_map/all_to_all | solution.py:131
  181.1 6.7 %copy-start = (bf16[768,2560]{1,0:T(8,128)(2,1)S(1)}, bf16[768,2560]{1,0:T(8,128)(2,1)}, u32[]{:S(2)}) copy-start(bf16[768,2560]{1,0:T(8,128)(2,1)} %reshape.389) | copy-start | bytes 11796484
  181.1 6.7 %copy-start.8 = (bf16[1,2560,768]{2,1,0:T(8,128)(2,1)S(1)}, bf16[1,2560,768]{2,1,0:T(8,128)(2,1)}, u32[]{:S(2)}) copy-start(bf16[1,2560,768]{2,1,0:T(8,128)(2,1)} %param.21) | copy-start | bytes 11796484
  187.7 3.5 %copy-start.9 = (bf16[1,768,2560]{2,1,0:T(8,128)(2,1)S(1)}, bf16[1,768,2560]{2,1,0:T(8,128)(2,1)}, u32[]{:S(2)}) copy-start(bf16[1,768,2560]{2,1,0:T(8,128)(2,1)} %param.23) | copy-start | bytes 11796484
  218.6 95.2 %all-to-all-start.3 = ((bf16[64,6,2,2560]{3,2,1,0:T(2,128)(2,1)}), bf16[64,6,2,2560]{3,2,1,0:T(2,128)(2,1)}, u32[]{:S(2)}, u32[]{:S(2)}) async-start(bf16[64,6,2,2560]{3,2,1,0:T(2,128)(2,1)} %reshape.390), calls=%async_computation.3 | async-start | bytes 7864320 | tf_op jit(solution)/shard_map/all_to_all | solution.py:149
where the time goes:
time: 320 us; the launch traced here: 319 us
  waiting for transfers between devices  187 us (58%)
  local copies, waits for them, and re-layouts  57.7 us (18%)
  matrix products  39.8 us (12%)
  starting transfers between devices  30.5 us (10%)
  other arithmetic  3.9 us (1%)
    all_to_all x1, waiting for transfers between devices, shards(): lax.all_to_all(result, 'expert', split_axis=0, concat_axis=0, tiled=True)  80.2 us
    all_to_all x1, waiting for transfers between devices, shards(): lax.all_to_all(packed_two, 'expert', split_axis=0, concat_axis=0, tiled=T...  66.6 us
    all_to_all x1, waiting for transfers between devices, shards(): lax.all_to_all(packed_one, 'expert', split_axis=0, concat_axis=0, tiled=T...  26 us
    dot_general x2, matrix products, expert_rows(): jnp.dot(hidden, down_mat, preferred_element_type=jnp.float32)  14 us
    all_to_all x1, waiting for transfers between devices, shards(): lax.all_to_all(result.reshape(received.shape), 'expert', split_axis=0, co...  13.9 us
    all_to_all x1, starting transfers between devices, shards(): lax.all_to_all(packed_one, 'expert', split_axis=0, concat_axis=0, tiled=T...  12 us
    reshape x2, local copies, waits for them, and re-layouts, shards(): received.reshape(-1, features)  11.3 us
    dot_general x2, matrix products, expert_rows(): gate_val = jnp.dot(rows, gate_mat, preferred_element_type=jnp.float32)  9.09 us
  transfers between devices with their start and end apart: 4, of which 4 were waited for; matrix products, arithmetic and copies ran while one was open for 27% of the time, Pallas kernels for 0%

commit v1 on v0

--- a/solution.py
+++ b/solution.py
@@ -2,9 +2,59 @@
 import jax.numpy as jnp
 from jax import lax
 from jax.sharding import PartitionSpec as P
+from jax.experimental import pallas as pl
+from jax.experimental.pallas import tpu as pltpu
 
 HEAD_WIDTH = 128
 CAP = 6
+
+
+def exchange_kernel(x_ref, o_ref, send_sem, recv_sem, local_sem):
+    me = lax.axis_index("expert")
+    width = x_ref.shape[0]
+
+    def remote(target, slot):
+        return pltpu.make_async_remote_copy(
+            src_ref=x_ref.at[target],
+            dst_ref=o_ref.at[slot],
+            send_sem=send_sem.at[target],
+            recv_sem=recv_sem.at[slot],
+            device_id={"expert": target},
+            device_id_type=pl.DeviceIdType.MESH,
+        )
+
+    local = pltpu.make_async_copy(x_ref.at[me], o_ref.at[me], local_sem)
+    local.start()
+
+    def start(step, carry):
+        remote(lax.rem(me + step, width), me).start()
+        return carry
+
+    lax.fori_loop(1, width, start, 0)
+
+    def finish(step, carry):
+        remote(lax.rem(me + step, width), me).wait_send()
+        remote(me, lax.rem(me + width - step, width)).wait_recv()
+        return carry
+
+    lax.fori_loop(1, width, finish, 0)
+    local.wait()
+
+
+def exchange(x):
+    width = x.shape[0]
+    return pl.pallas_call(
+        exchange_kernel,
+        out_shape=jax.ShapeDtypeStruct(x.shape, x.dtype),
+        in_specs=[pl.BlockSpec(memory_space=pl.ANY)],
+        out_specs=pl.BlockSpec(memory_space=pl.ANY),
+        scratch_shapes=[
+            pltpu.SemaphoreType.DMA((width,)),
+            pltpu.SemaphoreType.DMA((width,)),
+            pltpu.SemaphoreType.DMA,
+        ],
+        compiler_params=pltpu.CompilerParams(has_side_effects=True),
+    )(x)
 
 
 def attend(query, key_rows, value_rows, lengths):
@@ -128,9 +178,7 @@
         tiled=True,
     )
     result = expert_rows(received.reshape(-1, features), own_gate, own_up, own_down)
-    back_one = lax.all_to_all(
-        result.reshape(received.shape), "expert", split_axis=0, concat_axis=0, tiled=True
-    )
+    back_one = exchange(result.reshape(width, CAP, features)).reshape(width, CAP, 1, features)
     out_one = combine(attn_one, back_one, spot_one, kept_one, gates[0])
     attn_two = attend(query[1], keys[1], values[1], lengths[1, 0])
     normed_two = normalize(attn_two, norm_gain)

time: 320 us -> 341 us (1.066)
  Pallas kernels: 0 us -> 115 us
  waiting for transfers between devices: 187 us -> 97 us
  starting transfers between devices: 30.5 us -> 26.5 us
  local copies, waits for them, and re-layouts: 57.7 us -> 54.1 us
    pallas_call x0 -> x1, Pallas kernels: none -> 115 us  [exchange(): pl.pallas_call(exchange_kernel, out_shape=jax.ShapeDtypeStruct(x.shape, x...]
    all_to_all x1, waiting for transfers between devices: 80.2 us -> 0.01 us  [shards(): lax.all_to_all(result, 'expert', split_axis=0, concat_axis=0, tiled=True)]
    all_to_all x1, waiting for transfers between devices: 66.6 us -> 82.4 us  [shards(): lax.all_to_all(packed_two, 'expert', split_axis=0, concat_axis=0, tiled=T...]
    all_to_all x1 -> x0, waiting for transfers between devices: 13.9 us -> none  [shards(): lax.all_to_all(result.reshape(received.shape), 'expert', split_axis=0, co...]
    all_to_all x1, waiting for transfers between devices: 26 us -> 14.5 us  [shards(): lax.all_to_all(packed_one, 'expert', split_axis=0, concat_axis=0, tiled=T...]
    all_to_all x1, starting transfers between devices: 6.44 us -> 12.3 us  [shards(): lax.all_to_all(packed_two, 'expert', split_axis=0, concat_axis=0, tiled=T...]
    all_to_all x1 -> x0, starting transfers between devices: 5.66 us -> none  [shards(): lax.all_to_all(result.reshape(received.shape), 'expert', split_axis=0, co...]
    all_to_all x1, starting transfers between devices: 12 us -> 7.77 us  [shards(): lax.all_to_all(packed_one, 'expert', split_axis=0, concat_axis=0, tiled=T...]
  transfers between devices with their start and end apart: 4 -> 3, of which waited for: 4 -> 2; matrix products, arithmetic and copies ran while one was open for 27% -> 21% of each run, Pallas kernels for 0% -> 34%
where the time goes in v1:
time: 341 us; the launch traced here: 338 us
  Pallas kernels  115 us (34%)
  waiting for transfers between devices  97 us (28%)
  local copies, waits for them, and re-layouts  54.1 us (16%)
  matrix products  40.8 us (12%)
  starting transfers between devices  26.5 us (8%)
  other arithmetic  4.58 us (1%)
    pallas_call x1, Pallas kernels, exchange(): pl.pallas_call(exchange_kernel, out_shape=jax.ShapeDtypeStruct(x.shape, x...  115 us
    all_to_all x1, waiting for transfers between devices, shards(): lax.all_to_all(packed_two, 'expert', split_axis=0, concat_axis=0, tiled=T...  82.4 us
    all_to_all x1, waiting for transfers between devices, shards(): lax.all_to_all(packed_one, 'expert', split_axis=0, concat_axis=0, tiled=T...  14.5 us
    dot_general x2, matrix products, expert_rows(): jnp.dot(hidden, down_mat, preferred_element_type=jnp.float32)  14 us
    all_to_all x1, starting transfers between devices, shards(): lax.all_to_all(packed_two, 'expert', split_axis=0, concat_axis=0, tiled=T...  12.3 us
    reshape x2, local copies, waits for them, and re-layouts, shards(): received.reshape(-1, features)  11.3 us
    dot_general x2, matrix products, expert_rows(): gate_val = jnp.dot(rows, gate_mat, preferred_element_type=jnp.float32)  9.09 us
    reshape x1, local copies, waits for them, and re-layouts, shards(): expert_rows(received.reshape(-1, features), own_gate, own_up, own_down)  8.72 us
  transfers between devices with their start and end apart: 3, of which 2 were waited for; matrix products, arithmetic and copies ran while one was open for 21% of the time, Pallas kernels for 34%

profile of v1, /device:TPU:8, one launch (start us, length us, event | category | flops | bytes accessed | tf_op | source)
XLA Modules:
  0.0 338.4 jit_solution(98814043851742346)
XLA Ops:
  6.4 2.9 scatter_custom_fusion
  10.6 4.6 %gather_fusion = bf16[768,2560]{1,0:T(8,128)(2,1)} fusion(bf16[65,2560]{1,0:T(8,128)(2,1)S(1)} %concatenate.3, s32[1024]{0:T(1024)S(1)} %pad_clamp_fusion), kind=kCustom, calls=%fused_computation | custom fusion | bytes 7867392 | tf_op jit(solution)/shard_map/gather | solution.py:128
  15.2 8.7 %reshape.393 = bf16[64,6,2,2560]{3,2,1,0:T(2,128)(2,1)} reshape(bf16[768,2560]{1,0:T(8,128)(2,1)} %gather_fusion) | data formatting | bytes 7864320 | tf_op jit(solution)/shard_map/reshape | solution.py:128
  23.9 12.3 %all-to-all-start.1 = ((bf16[64,6,2,2560]{3,2,1,0:T(2,128)(2,1)}), bf16[64,6,2,2560]{3,2,1,0:T(2,128)(2,1)}, u32[]{:S(2)}, u32[]{:S(2)}) async-start(bf16[64,6,2,2560]{3,2,1,0:T(2,128)(2,1)} %reshape.393), calls=%async_computation.1 | async-start | bytes 7864320 | tf_op jit(solution)/shard_map/all_to_all | solution.py:187
  40.3 3.3 copy.95
  43.6 82.4 %all-to-all-done.1 = bf16[64,6,2,2560]{3,2,1,0:T(2,128)(2,1)} async-done(((bf16[64,6,2,2560]{3,2,1,0:T(2,128)(2,1)}), bf16[64,6,2,2560]{3,2,1,0:T(2,128)(2,1)}, u32[]{:S(2)}, u32[]{:S(2)}) %all-to-all-start.1) | async-done | bytes 3932192 | tf_op jit(solution)/shard_map/all_to_all | solution.py:187
  126.0 7.8 %all-to-all-start = ((bf16[64,3,2,2560]{3,2,1,0:T(2,128)(2,1)}), bf16[64,3,2,2560]{3,2,1,0:T(2,128)(2,1)S(1)}, u32[]{:S(2)}, u32[]{:S(2)}) async-start(bf16[64,3,2,2560]{3,2,1,0:T(2,128)(2,1)} %copy.95), calls=%async_computation | async-start | bytes 3932160 | tf_op jit(solution)/shard_map/all_to_all | solution.py:173
  133.8 9.0 %reshape.394 = bf16[768,2560]{1,0:T(8,128)(2,1)} reshape(bf16[64,6,2,2560]{3,2,1,0:T(2,128)(2,1)} %all-to-all-done.1) | data formatting | bytes 7864320 | tf_op jit(solution)/shard_map/reshape | solution.py:194
  142.9 6.6 %fusion.4 = f32[768,768]{1,0:T(8,128)S(1)} fusion(bf16[768,2560]{1,0:T(8,128)(2,1)} %reshape.394, bf16[1,2560,768]{2,1,0:T(8,128)(2,1)} %param.22), kind=kOutput, calls=%fused_computation.9 | convolution fusion | flops 3019898880 | bytes 10223616 | tf_op jit(solution)/shard_map/dot_general | solution.py:89
  149.5 3.4 %multiply_convert_fusion = bf16[768,768]{1,0:T(8,128)(2,1)S(1)} fusion(f32[768,768]{1,0:T(8,128)S(1)} %fusion.4, bf16[768,2560]{1,0:T(8,128)(2,1)S(1)} %copy-done, bf16[1,2560,768]{2,1,0:T(8,128)(2,1)S(1)} %copy-done.7), kind=kOutput, calls=%fused_computation.27 | convolution fusion | flops 3023437824 | bytes 11403264 | tf_op jit(solution)/shard_map/dot_general | solution.py:88
  153.0 4.8 %convolution_convert_fusion = bf16[768,2560]{1,0:T(8,128)(2,1)} fusion(bf16[768,768]{1,0:T(8,128)(2,1)S(1)} %multiply_convert_fusion, bf16[1,768,2560]{2,1,0:T(8,128)(2,1)S(1)} %copy-done.8), kind=kOutput, calls=%fused_computation.4 | convolution fusion | flops 3021864960 | bytes 9043968 | tf_op jit(solution)/shard_map/dot_general | solution.py:91
  157.8 8.7 %reshape.395 = bf16[64,6,2,2560]{3,2,1,0:T(2,128)(2,1)} reshape(bf16[768,2560]{1,0:T(8,128)(2,1)} %convolution_convert_fusion) | data formatting | bytes 7864320 | tf_op jit(solution)/shard_map/reshape | solution.py:194
  166.5 14.5 %all-to-all-done = bf16[64,3,2,2560]{3,2,1,0:T(2,128)(2,1)S(1)} async-done(((bf16[64,3,2,2560]{3,2,1,0:T(2,128)(2,1)}), bf16[64,3,2,2560]{3,2,1,0:T(2,128)(2,1)S(1)}, u32[]{:S(2)}, u32[]{:S(2)}) %all-to-all-start) | async-done | bytes 1966112 | tf_op jit(solution)/shard_map/all_to_all | solution.py:173
  181.0 6.4 %all-to-all-start.2 = ((bf16[64,6,2,2560]{3,2,1,0:T(2,128)(2,1)}), bf16[64,6,2,2560]{3,2,1,0:T(2,128)(2,1)}, u32[]{:S(2)}, u32[]{:S(2)}) async-start(bf16[64,6,2,2560]{3,2,1,0:T(2,128)(2,1)} %reshape.395), calls=%async_computation.2 | async-start | bytes 7864320 | tf_op jit(solution)/shard_map/all_to_all | solution.py:197
  187.5 1.5 copy.88
  189.3 1.4 reshape.384
  191.6 1.8 copy.105
  193.4 2.3 reshape.387
  195.7 5.7 %fusion.10 = f32[384,768]{1,0:T(8,128)} fusion(bf16[384,2560]{1,0:T(8,128)(2,1)} %reshape.387, bf16[1,2560,768]{2,1,0:T(8,128)(2,1)} %param.21), kind=kOutput, calls=%fused_computation.15 | convolution fusion | flops 1509949440 | bytes 7077888 | tf_op jit(solution)/shard_map/dot_general | solution.py:88
  201.4 9.2 %convolution_convert_fusion.1 = bf16[384,2560]{1,0:T(8,128)(2,1)} fusion(bf16[1,768,2560]{2,1,0:T(8,128)(2,1)} %param.23, bf16[384,2560]{1,0:T(8,128)(2,1)S(1)} %copy-done.1, bf16[1,2560,768]{2,1,0:T(8,128)(2,1)} %param.22, f32[384,768]{1,0:T(8,128)} %fusion.10), kind=kOutput, calls=%fused_computation.5 | convolution fusion | flops 3022651392 | bytes 12976128 | tf_op jit(solution)/shard_map/dot_general | solution.py:91
  210.5 4.1 %reshape.388.x_ref = bf16[64,6,2560]{2,1,0:T(8,128)(2,1)} reshape(bf16[384,2560]{1,0:T(8,128)(2,1)} %convolution_convert_fusion.1) | data formatting | bytes 3932160 | tf_op jit(solution)/shard_map/reshape | solution.py:181
  214.7 115.0 %shard_map.118 = bf16[64,6,2560]{2,1,0:T(8,128)(2,1)} custom-call(bf16[64,6,2560]{2,1,0:T(8,128)(2,1)} %reshape.388.x_ref), custom_call_target="tpu_custom_call" | custom-call | tf_op jit(solution)/shard_map/pallas_call | solution.py:46
  329.7 3.3 fusion.25
  333.1 4.5 %fusion.26 = bf16[1,64,2560]{2,1,0:T(8,128)(2,1)S(1)} fusion(f32[64,2560]{1,0:T(8,128)S(1)} %reshape.391, bf16[64,6,2,2560]{3,2,1,0:T(2,128)(2,1)} %all-to-all-done.2, f32[64,64,6,2]{0,3,2,1:T(2,128)S(1)} %bitcast.122), kind=kOutput, calls=%fused_computation.26 | convolution fusion | flops 1510277120 | bytes 5111808 | tf_op jit(solution)/shard_map/tabc,abcf->tf/dot_general | solution.py:136
  (88 shorter events, 13.6 us)
Async XLA Ops:
  0.0 4.4 %copy-start.5 = (s32[2,64,6]{1,0,2:T(2,128)S(1)}, s32[2,64,6]{1,0,2:T(2,128)}, u32[]{:S(2)}) copy-start(s32[2,64,6]{1,0,2:T(2,128)} %param.16) | copy-start | bytes 9220
  0.0 4.9 %copy-start.9 = (s32[4]{0:T(128)S(1)}, s32[4]{0:T(128)}, u32[]{:S(2)}) copy-start(s32[4]{0:T(128)} %param.20) | copy-start | bytes 52
  0.0 5.0 %copy-start.10 = (s32[64]{0:T(128)S(1)}, s32[64]{0:T(128)}, u32[]{:S(2)}) copy-start(s32[64]{0:T(128)} %param.19) | copy-start | bytes 772
  0.0 5.1 %copy-start.3 = (bf16[2,64,512]{2,1,0:T(8,128)(2,1)S(1)}, bf16[2,64,512]{2,1,0:T(8,128)(2,1)}, u32[]{:S(2)}) copy-start(bf16[2,64,512]{2,1,0:T(8,128)(2,1)} %param.14) | copy-start | bytes 393220
  9.4 1.1 copy-start.4
  23.9 12.3 %copy-start.6 = (f32[2,64,6]{1,0,2:T(2,128)S(1)}, f32[2,64,6]{1,0,2:T(2,128)}, u32[]{:S(2)}) copy-start(f32[2,64,6]{1,0,2:T(2,128)} %param.17) | copy-start | bytes 9220
  23.9 102.1 %all-to-all-start.1 = ((bf16[64,6,2,2560]{3,2,1,0:T(2,128)(2,1)}), bf16[64,6,2,2560]{3,2,1,0:T(2,128)(2,1)}, u32[]{:S(2)}, u32[]{:S(2)}) async-start(bf16[64,6,2,2560]{3,2,1,0:T(2,128)(2,1)} %reshape.393), calls=%async_computation.1 | async-start | bytes 7864320 | tf_op jit(solution)/shard_map/all_to_all | solution.py:187
  126.0 55.0 %all-to-all-start = ((bf16[64,3,2,2560]{3,2,1,0:T(2,128)(2,1)}), bf16[64,3,2,2560]{3,2,1,0:T(2,128)(2,1)S(1)}, u32[]{:S(2)}, u32[]{:S(2)}) async-start(bf16[64,3,2,2560]{3,2,1,0:T(2,128)(2,1)} %copy.95), calls=%async_computation | async-start | bytes 3932160 | tf_op jit(solution)/shard_map/all_to_all | solution.py:173
  142.9 6.7 %copy-start = (bf16[768,2560]{1,0:T(8,128)(2,1)S(1)}, bf16[768,2560]{1,0:T(8,128)(2,1)}, u32[]{:S(2)}) copy-start(bf16[768,2560]{1,0:T(8,128)(2,1)} %reshape.394) | copy-start | bytes 11796484
  142.9 6.7 %copy-start.7 = (bf16[1,2560,768]{2,1,0:T(8,128)(2,1)S(1)}, bf16[1,2560,768]{2,1,0:T(8,128)(2,1)}, u32[]{:S(2)}) copy-start(bf16[1,2560,768]{2,1,0:T(8,128)(2,1)} %param.21) | copy-start | bytes 11796484
  149.5 3.5 %copy-start.8 = (bf16[1,768,2560]{2,1,0:T(8,128)(2,1)S(1)}, bf16[1,768,2560]{2,1,0:T(8,128)(2,1)}, u32[]{:S(2)}) copy-start(bf16[1,768,2560]{2,1,0:T(8,128)(2,1)} %param.23) | copy-start | bytes 11796484
  181.0 152.0 %all-to-all-start.2 = ((bf16[64,6,2,2560]{3,2,1,0:T(2,128)(2,1)}), bf16[64,6,2,2560]{3,2,1,0:T(2,128)(2,1)}, u32[]{:S(2)}, u32[]{:S(2)}) async-start(bf16[64,6,2,2560]{3,2,1,0:T(2,128)(2,1)} %reshape.395), calls=%async_computation.2 | async-start | bytes 7864320 | tf_op jit(solution)/shard_map/all_to_all | solution.py:197
  195.7 5.7 %copy-start.1 = (bf16[384,2560]{1,0:T(8,128)(2,1)S(1)}, bf16[384,2560]{1,0:T(8,128)(2,1)}, u32[]{:S(2)}) copy-start(bf16[384,2560]{1,0:T(8,128)(2,1)} %reshape.387) | copy-start | bytes 5898244
  329.7 3.3 copy-start.2

commit v2 on v0

--- a/solution.py
+++ b/solution.py
@@ -117,34 +117,44 @@
     doubled = jnp.sum((dup_experts[:, None] == expert_list[None, :]).astype(jnp.int32), axis=0)
     own_gate, own_up, own_down = (w_gate[0], w_up[0], w_down[0])
     attn_one = attend(query[0], keys[0], values[0], lengths[0, 0])
+    attn_two = attend(query[1], keys[1], values[1], lengths[1, 0])
     normed_one = normalize(attn_one, norm_gain)
+    normed_two = normalize(attn_two, norm_gain)
     flat_one, kept_one = routing(routes[0], jnp.ones_like(doubled), holder, holder, 1)
-    packed_one, spot_one = pack(normed_one, flat_one, kept_one, (width, CAP // 2, 2))
-    received = lax.all_to_all(
-        packed_one,
-        "expert",
-        split_axis=0,
-        concat_axis=0,
-        tiled=True,
+    flat_two, kept_two = routing(routes[1], 1 + doubled, holder, holder, 2)
+    per_dest = 3 * CAP
+    slots = width * per_dest
+    spot_one = jnp.where(kept_one, flat_one, width * CAP)
+    spot_two = jnp.where(kept_two, flat_two, width * 2 * CAP)
+    merged_one = jnp.where(kept_one, (flat_one // CAP) * per_dest + flat_one % CAP, slots)
+    merged_two = jnp.where(
+        kept_two, (flat_two // (2 * CAP)) * per_dest + CAP + flat_two % (2 * CAP), slots
     )
-    result = expert_rows(received.reshape(-1, features), own_gate, own_up, own_down)
+    slot_list = lax.iota(jnp.int32, slots)[:, None, None]
+    picker = jnp.concatenate(
+        [
+            jnp.any(merged_one[None, :, :] == slot_list, axis=2),
+            jnp.any(merged_two[None, :, :] == slot_list, axis=2),
+        ],
+        axis=1,
+    ).astype(normed_one.dtype)
+    normed = jnp.concatenate([normed_one, normed_two], axis=0)
+    packed = jnp.einsum(
+        "abct,tf->abcf",
+        picker.reshape(width, per_dest // 2, 2, -1),
+        normed,
+        preferred_element_type=jnp.float32,
+    ).astype(normed.dtype)
+    received = lax.all_to_all(packed, "expert", split_axis=0, concat_axis=0, tiled=True)
+    received_one = received[:, : CAP // 2]
+    received_two = received[:, CAP // 2 :]
+    result = expert_rows(received_one.reshape(-1, features), own_gate, own_up, own_down)
     back_one = lax.all_to_all(
-        result.reshape(received.shape), "expert", split_axis=0, concat_axis=0, tiled=True
+        result.reshape(received_one.shape), "expert", split_axis=0, concat_axis=0, tiled=True
     )
     out_one = combine(attn_one, back_one, spot_one, kept_one, gates[0])
-    attn_two = attend(query[1], keys[1], values[1], lengths[1, 0])
-    normed_two = normalize(attn_two, norm_gain)
-    flat_two, kept_two = routing(routes[1], 1 + doubled, holder, holder, 2)
-    packed_two, spot_two = gather_pack(normed_two, flat_two, kept_two, (width, CAP, 2))
-    received = lax.all_to_all(
-        packed_two,
-        "expert",
-        split_axis=0,
-        concat_axis=0,
-        tiled=True,
-    )
-    result = expert_rows(received.reshape(-1, features), own_gate, own_up, own_down).reshape(
-        received.shape
+    result = expert_rows(received_two.reshape(-1, features), own_gate, own_up, own_down).reshape(
+        received_two.shape
     )
     back_two = lax.all_to_all(result, "expert", split_axis=0, concat_axis=0, tiled=True)
     out_two = combine(attn_two, back_two, spot_two, kept_two, gates[1])

time: 320 us -> 374 us (1.17)
  blocking collectives: 0 us -> 144 us
  waiting for transfers between devices: 187 us -> 90.1 us
  local copies, waits for them, and re-layouts: 57.7 us -> 78.2 us
  starting transfers between devices: 30.5 us -> 12 us
    all_to_all x0 -> x1, blocking collectives: none -> 144 us  [shards(): lax.all_to_all(packed, 'expert', split_axis=0, concat_axis=0, tiled=True)]
    all_to_all x3 -> x1, waiting for transfers between devices: 106 us -> 7.83 us  [shards(): lax.all_to_all(result.reshape(received_one.shape), 'expert', split_axis=0...]
    convert_element_type x3 -> x1, local copies, waits for them, and re-layouts: 3.92 us -> 35 us  [shards(): packed = jnp.einsum('abct,tf->abcf', picker.reshape(width, per_dest // 2,...]
    all_to_all x3 -> x1, starting transfers between devices: 24.1 us -> 5.59 us  [shards(): lax.all_to_all(result.reshape(received_one.shape), 'expert', split_axis=0...]
    reshape x6 -> x5, local copies, waits for them, and re-layouts: 33.9 us -> 25.1 us  [the longest x1 9.04 us: shards(): received_two.reshape(-1, features)]
    slice x0 -> x2, local copies, waits for them, and re-layouts: none -> 8.12 us  [the longest x1 6.77 us: shards(): received_two = received[:, CAP // 2:]]
    gather x1 -> x0, local copies, waits for them, and re-layouts: 4.63 us -> none  [gather_pack(): return (padded[source_row].reshape(shape + (normed.shape[1],)), spot)]
  transfers between devices with their start and end apart: 4 -> 2, of which waited for: 4 -> 2; matrix products, arithmetic and copies ran while one was open for 27% -> 12% of each run, Pallas kernels for 0% -> 0%
where the time goes in v2:
time: 374 us; the launch traced here: 373 us
  blocking collectives  144 us (39%)
  waiting for transfers between devices  90.1 us (24%)
  local copies, waits for them, and re-layouts  78.2 us (21%)
  matrix products  42.7 us (11%)
  starting transfers between devices  12 us (3%)
  other arithmetic  5.63 us (2%)
    all_to_all x1, blocking collectives, shards(): lax.all_to_all(packed, 'expert', split_axis=0, concat_axis=0, tiled=True)  144 us
    all_to_all x1, waiting for transfers between devices, shards(): lax.all_to_all(result, 'expert', split_axis=0, concat_axis=0, tiled=True)  82.3 us
    convert_element_type x1, local copies, waits for them, and re-layouts, shards(): packed = jnp.einsum('abct,tf->abcf', picker.reshape(width, per_dest // 2,...  35 us
    dot_general x2, matrix products, expert_rows(): jnp.dot(hidden, down_mat, preferred_element_type=jnp.float32)  14 us
    dot_general x2, matrix products, expert_rows(): gate_val = jnp.dot(rows, gate_mat, preferred_element_type=jnp.float32)  9.09 us
    reshape x1, local copies, waits for them, and re-layouts, shards(): received_two.reshape(-1, features)  9.04 us
    reshape x1, local copies, waits for them, and re-layouts, shards(): expert_rows(received_two.reshape(-1, features), own_gate, own_up, own_down)  8.72 us
    all_to_all x1, waiting for transfers between devices, shards(): lax.all_to_all(result.reshape(received_one.shape), 'expert', split_axis=0...  7.83 us
  transfers between devices with their start and end apart: 2, of which 2 were waited for; matrix products, arithmetic and copies ran while one was open for 12% of the time, Pallas kernels for 0%

profile of v2, /device:TPU:8, one launch (start us, length us, event | category | flops | bytes accessed | tf_op | source)
XLA Modules:
  0.0 373.2 jit_solution(13894181418758451678)
XLA Ops:
  4.5 1.3 fusion.45
  10.2 1.7 multiply_reduce_fusion
  12.8 1.7 convolution_convert_fusion
  14.5 35.0 %copy.99 = bf16[64,9,2,2560]{3,2,1,0:T(2,128)(2,1)S(1)} copy(bf16[64,9,2,2560]{3,0,2,1:T(8,128)(2,1)S(1)} %convolution_convert_fusion) | data formatting | bytes 11796480 | tf_op jit(solution)/shard_map/convert_element_type | solution.py:147
  49.5 144.2 %all_to_all.15 = bf16[64,9,2,2560]{3,2,1,0:T(2,128)(2,1)S(1)} all-to-all(bf16[64,9,2,2560]{3,2,1,0:T(2,128)(2,1)S(1)} %copy.99), channel_id=1, replica_groups=mesh['dp'=4,'expert'=64] {'expert'}, dimensions={0} | all-to-all | bytes 11796480 | tf_op jit(solution)/shard_map/all_to_all | solution.py:148
  193.6 2.5 copy-done
  196.1 1.3 slice.56
  197.5 2.2 reshape.354
  199.7 5.7 %fusion.10 = f32[384,768]{1,0:T(8,128)} fusion(bf16[384,2560]{1,0:T(8,128)(2,1)} %reshape.354, bf16[1,2560,768]{2,1,0:T(8,128)(2,1)} %param.21), kind=kOutput, calls=%fused_computation.13 | convolution fusion | flops 1509949440 | bytes 7077888 | tf_op jit(solution)/shard_map/dot_general | solution.py:38
  205.4 9.2 %convolution_convert_fusion.2 = bf16[384,2560]{1,0:T(8,128)(2,1)} fusion(bf16[1,768,2560]{2,1,0:T(8,128)(2,1)} %param.23, bf16[384,2560]{1,0:T(8,128)(2,1)S(1)} %copy-done.2, bf16[1,2560,768]{2,1,0:T(8,128)(2,1)} %param.22, f32[384,768]{1,0:T(8,128)} %fusion.10), kind=kOutput, calls=%fused_computation.4 | convolution fusion | flops 3022651392 | bytes 12976128 | tf_op jit(solution)/shard_map/dot_general | solution.py:41
  214.5 5.0 %reshape.355 = bf16[64,3,2,2560]{3,2,1,0:T(2,128)(2,1)} reshape(bf16[384,2560]{1,0:T(8,128)(2,1)} %convolution_convert_fusion.2) | data formatting | bytes 3932160 | tf_op jit(solution)/shard_map/reshape | solution.py:153
  219.6 5.6 %all-to-all-start.1 = ((bf16[64,3,2,2560]{3,2,1,0:T(2,128)(2,1)}), bf16[64,3,2,2560]{3,2,1,0:T(2,128)(2,1)S(1)}, u32[]{:S(2)}, u32[]{:S(2)}) async-start(bf16[64,3,2,2560]{3,2,1,0:T(2,128)(2,1)} %reshape.355), calls=%async_computation.1 | async-start | bytes 3932160 | tf_op jit(solution)/shard_map/all_to_all | solution.py:152
  225.1 6.8 %slice.57 = bf16[64,6,2,2560]{3,2,1,0:T(2,128)(2,1)} slice(bf16[64,9,2,2560]{3,2,1,0:T(2,128)(2,1)} %copy-done), slice={[0:64], [3:9], [0:2], [0:2560]} | slice | bytes 7864320 | tf_op jit(solution)/shard_map/slice | solution.py:150
  231.9 9.0 %reshape.357 = bf16[768,2560]{1,0:T(8,128)(2,1)} reshape(bf16[64,6,2,2560]{3,2,1,0:T(2,128)(2,1)} %slice.57) | data formatting | bytes 7864320 | tf_op jit(solution)/shard_map/reshape | solution.py:156
  241.0 6.6 %fusion.4 = f32[768,768]{1,0:T(8,128)S(1)} fusion(bf16[768,2560]{1,0:T(8,128)(2,1)} %reshape.357, bf16[1,2560,768]{2,1,0:T(8,128)(2,1)} %param.22), kind=kOutput, calls=%fused_computation.7 | convolution fusion | flops 3019898880 | bytes 10223616 | tf_op jit(solution)/shard_map/dot_general | solution.py:39
  247.6 3.4 multiply_convert_fusion
  251.1 4.8 %convolution_convert_fusion.1 = bf16[768,2560]{1,0:T(8,128)(2,1)} fusion(bf16[768,768]{1,0:T(8,128)(2,1)S(1)} %multiply_convert_fusion, bf16[1,768,2560]{2,1,0:T(8,128)(2,1)S(1)} %copy-done.10), kind=kOutput, calls=%fused_computation.3 | convolution fusion | flops 3021864960 | bytes 9043968 | tf_op jit(solution)/shard_map/dot_general | solution.py:41
  255.9 8.7 %reshape.358 = bf16[64,6,2,2560]{3,2,1,0:T(2,128)(2,1)} reshape(bf16[768,2560]{1,0:T(8,128)(2,1)} %convolution_convert_fusion.1) | data formatting | bytes 7864320 | tf_op jit(solution)/shard_map/reshape | solution.py:156
  264.6 7.8 %all-to-all-done.1 = bf16[64,3,2,2560]{3,2,1,0:T(2,128)(2,1)S(1)} async-done(((bf16[64,3,2,2560]{3,2,1,0:T(2,128)(2,1)}), bf16[64,3,2,2560]{3,2,1,0:T(2,128)(2,1)S(1)}, u32[]{:S(2)}, u32[]{:S(2)}) %all-to-all-start.1) | async-done | bytes 1966112 | tf_op jit(solution)/shard_map/all_to_all | solution.py:152
  272.4 6.4 %all-to-all-start.2 = ((bf16[64,6,2,2560]{3,2,1,0:T(2,128)(2,1)}), bf16[64,6,2,2560]{3,2,1,0:T(2,128)(2,1)}, u32[]{:S(2)}, u32[]{:S(2)}) async-start(bf16[64,6,2,2560]{3,2,1,0:T(2,128)(2,1)} %reshape.358), calls=%async_computation.2 | async-start | bytes 7864320 | tf_op jit(solution)/shard_map/all_to_all | solution.py:159
  281.6 1.8 copy.103
  283.5 1.9 fusion.25
  285.3 82.3 %all-to-all-done.2 = bf16[64,6,2,2560]{3,2,1,0:T(2,128)(2,1)} async-done(((bf16[64,6,2,2560]{3,2,1,0:T(2,128)(2,1)}), bf16[64,6,2,2560]{3,2,1,0:T(2,128)(2,1)}, u32[]{:S(2)}, u32[]{:S(2)}) %all-to-all-start.2) | async-done | bytes 3932192 | tf_op jit(solution)/shard_map/all_to_all | solution.py:159
  367.6 4.6 %fusion.26 = bf16[1,64,2560]{2,1,0:T(8,128)(2,1)S(1)} fusion(f32[64,2560]{1,0:T(8,128)S(1)} %reshape.353, bf16[64,6,2,2560]{3,2,1,0:T(2,128)(2,1)} %all-to-all-done.2, f32[64,64,6,2]{0,3,2,1:T(2,128)} %bitcast.103), kind=kOutput, calls=%fused_computation.24 | convolution fusion | flops 1510277120 | bytes 5111808 | tf_op jit(solution)/shard_map/tabc,abcf->tf/dot_general | solution.py:86
  (79 shorter events, 13.2 us)
Async XLA Ops:
  0.0 2.4 copy-start.8
  3.2 3.0 copy-start.6
  3.7 3.0 copy-start.11
  3.7 3.1 copy-start.12
  4.1 4.9 %copy-start.4 = (bf16[2,64,512]{2,1,0:T(8,128)(2,1)S(1)}, bf16[2,64,512]{2,1,0:T(8,128)(2,1)}, u32[]{:S(2)}) copy-start(bf16[2,64,512]{2,1,0:T(8,128)(2,1)} %param.14) | copy-start | bytes 393220
  11.9 0.7 copy-start.5
  193.6 2.5 copy-start
  199.7 5.7 %copy-start.2 = (bf16[384,2560]{1,0:T(8,128)(2,1)S(1)}, bf16[384,2560]{1,0:T(8,128)(2,1)}, u32[]{:S(2)}) copy-start(bf16[384,2560]{1,0:T(8,128)(2,1)} %reshape.354) | copy-start | bytes 5898244
  219.6 52.9 %all-to-all-start.1 = ((bf16[64,3,2,2560]{3,2,1,0:T(2,128)(2,1)}), bf16[64,3,2,2560]{3,2,1,0:T(2,128)(2,1)S(1)}, u32[]{:S(2)}, u32[]{:S(2)}) async-start(bf16[64,3,2,2560]{3,2,1,0:T(2,128)(2,1)} %reshape.355), calls=%async_computation.1 | async-start | bytes 3932160 | tf_op jit(solution)/shard_map/all_to_all | solution.py:152
  241.0 6.7 %copy-start.1 = (bf16[768,2560]{1,0:T(8,128)(2,1)S(1)}, bf16[768,2560]{1,0:T(8,128)(2,1)}, u32[]{:S(2)}) copy-start(bf16[768,2560]{1,0:T(8,128)(2,1)} %reshape.357) | copy-start | bytes 11796484
  241.0 6.7 %copy-start.9 = (bf16[1,2560,768]{2,1,0:T(8,128)(2,1)S(1)}, bf16[1,2560,768]{2,1,0:T(8,128)(2,1)}, u32[]{:S(2)}) copy-start(bf16[1,2560,768]{2,1,0:T(8,128)(2,1)} %param.21) | copy-start | bytes 11796484
  247.6 3.5 copy-start.10
  264.6 14.3 %copy-start.7 = (f32[2,64,6]{1,0,2:T(2,128)S(1)}, f32[2,64,6]{1,0,2:T(2,128)}, u32[]{:S(2)}) copy-start(f32[2,64,6]{1,0,2:T(2,128)} %param.17) | copy-start | bytes 9220
  272.4 95.2 %all-to-all-start.2 = ((bf16[64,6,2,2560]{3,2,1,0:T(2,128)(2,1)}), bf16[64,6,2,2560]{3,2,1,0:T(2,128)(2,1)}, u32[]{:S(2)}, u32[]{:S(2)}) async-start(bf16[64,6,2,2560]{3,2,1,0:T(2,128)(2,1)} %reshape.358), calls=%async_computation.2 | async-start | bytes 7864320 | tf_op jit(solution)/shard_map/all_to_all | solution.py:159
  367.6 4.6 %copy-start.3 = (bf16[1,64,2560]{2,1,0:T(8,128)(2,1)S(1)}, bf16[1,64,2560]{2,1,0:T(8,128)(2,1)}, u32[]{:S(2)}) copy-start(bf16[1,64,2560]{2,1,0:T(8,128)(2,1)} %fusion.25) | copy-start | bytes 983044

commit v3 on v0

--- a/solution.py
+++ b/solution.py
@@ -2,6 +2,8 @@
 import jax.numpy as jnp
 from jax import lax
 from jax.sharding import PartitionSpec as P
+from jax.experimental import pallas as pl
+from jax.experimental.pallas import tpu as pltpu
 
 HEAD_WIDTH = 128
 CAP = 6
@@ -29,6 +31,58 @@
     return mixed.reshape(rows, kv_heads * query_group * HEAD_WIDTH)
 
 
+def attend_kernel(query_ref, key_ref, value_ref, ends_ref, gain_ref, attn_ref, normed_ref):
+    rows = query_ref.shape[0]
+    kv_heads = key_ref.shape[1] // HEAD_WIDTH
+    query_group = query_ref.shape[1] // HEAD_WIDTH // kv_heads
+    ends = ends_ref[...]
+    position = lax.broadcasted_iota(jnp.int32, (rows, ends.shape[1]), 0)
+    request = jnp.sum((position >= ends).astype(jnp.int32), axis=1, keepdims=True)
+    row = lax.broadcasted_iota(jnp.int32, (rows, rows), 0)
+    col = lax.broadcasted_iota(jnp.int32, (rows, rows), 1)
+    request_col = jnp.sum(
+        (lax.broadcasted_iota(jnp.int32, (ends.shape[1], rows), 1) >= ends.reshape(-1, 1)).astype(
+            jnp.int32
+        ),
+        axis=0,
+        keepdims=True,
+    )
+    allowed = (request == request_col) & (col <= row)
+    for head in range(kv_heads * query_group):
+        kv = head // query_group
+        q = query_ref[:, head * HEAD_WIDTH : (head + 1) * HEAD_WIDTH]
+        k = key_ref[:, kv * HEAD_WIDTH : (kv + 1) * HEAD_WIDTH]
+        v = value_ref[:, kv * HEAD_WIDTH : (kv + 1) * HEAD_WIDTH]
+        logits = lax.dot_general(
+            q, k, (((1,), (1,)), ((), ())), preferred_element_type=jnp.float32
+        ) * HEAD_WIDTH ** (-0.5)
+        logits = jnp.where(allowed, logits, -1e30)
+        highest = jnp.max(logits, axis=-1, keepdims=True)
+        weights = jnp.exp(logits - highest)
+        probs = (weights / jnp.sum(weights, axis=-1, keepdims=True)).astype(jnp.bfloat16)
+        attn_ref[:, head * HEAD_WIDTH : (head + 1) * HEAD_WIDTH] = jnp.dot(
+            probs, v, preferred_element_type=jnp.float32
+        )
+    attn = attn_ref[...]
+    meansq = jnp.mean(attn * attn, axis=-1, keepdims=True)
+    normed_ref[...] = (attn * lax.rsqrt(meansq + 1e-05) * gain_ref[...]).astype(jnp.bfloat16)
+
+
+def attend_normed(query, key_rows, value_rows, lengths, gain):
+    rows, features = query.shape
+    ends = jnp.cumsum(lengths).reshape(1, -1)
+    vmem = pl.BlockSpec(memory_space=pltpu.VMEM)
+    return pl.pallas_call(
+        attend_kernel,
+        out_shape=(
+            jax.ShapeDtypeStruct((rows, features), jnp.float32),
+            jax.ShapeDtypeStruct((rows, features), jnp.bfloat16),
+        ),
+        in_specs=[vmem] * 5,
+        out_specs=(vmem, vmem),
+    )(query, key_rows, value_rows, ends, gain.reshape(1, -1))
+
+
 def normalize(attn, gain):
     meansq = jnp.mean(attn * attn, axis=-1, keepdims=True)
     return (attn * lax.rsqrt(meansq + 1e-05) * gain).astype(jnp.bfloat16)
@@ -116,8 +170,7 @@
     )
     doubled = jnp.sum((dup_experts[:, None] == expert_list[None, :]).astype(jnp.int32), axis=0)
     own_gate, own_up, own_down = (w_gate[0], w_up[0], w_down[0])
-    attn_one = attend(query[0], keys[0], values[0], lengths[0, 0])
-    normed_one = normalize(attn_one, norm_gain)
+    attn_one, normed_one = attend_normed(query[0], keys[0], values[0], lengths[0, 0], norm_gain)
     flat_one, kept_one = routing(routes[0], jnp.ones_like(doubled), holder, holder, 1)
     packed_one, spot_one = pack(normed_one, flat_one, kept_one, (width, CAP // 2, 2))
     received = lax.all_to_all(
@@ -132,8 +185,7 @@
         result.reshape(received.shape), "expert", split_axis=0, concat_axis=0, tiled=True
     )
     out_one = combine(attn_one, back_one, spot_one, kept_one, gates[0])
-    attn_two = attend(query[1], keys[1], values[1], lengths[1, 0])
-    normed_two = normalize(attn_two, norm_gain)
+    attn_two, normed_two = attend_normed(query[1], keys[1], values[1], lengths[1, 0], norm_gain)
     flat_two, kept_two = routing(routes[1], 1 + doubled, holder, holder, 2)
     packed_two, spot_two = gather_pack(normed_two, flat_two, kept_two, (width, CAP, 2))
     received = lax.all_to_all(

time: 320 us -> 334 us (1.044)
  Pallas kernels: 0 us -> 16.2 us
  matrix products: 39.8 us -> 35.6 us
  local copies, waits for them, and re-layouts: 57.7 us -> 53.7 us
    pallas_call x0 -> x2, Pallas kernels: none -> 16.2 us  [attend_normed(): pl.pallas_call(attend_kernel, out_shape=(jax.ShapeDtypeStruct((rows, feat...]
    all_to_all x1, waiting for transfers between devices: 80.2 us -> 86.9 us  [shards(): lax.all_to_all(result, 'expert', split_axis=0, concat_axis=0, tiled=True)]
    all_to_all x1, waiting for transfers between devices: 26 us -> 21.5 us  [shards(): lax.all_to_all(packed_one, 'expert', split_axis=0, concat_axis=0, tiled=T...]
    transpose x2 -> x0, local copies, waits for them, and re-layouts: 3.98 us -> none  [attend(): jnp.einsum('hgqk,khd->qhgd', probs, value_heads, preferred_element_type=j...]
    squeeze x0 -> x2, local copies, waits for them, and re-layouts: none -> 3.61 us  [the longest x1 1.95 us: shards(): query[0]]
  transfers between devices with their start and end apart: 4 -> 4, of which waited for: 4 -> 4; matrix products, arithmetic and copies ran while one was open for 27% -> 22% of each run, Pallas kernels for 0% -> 2%
where the time goes in v3:
time: 334 us; the launch traced here: 333 us
  waiting for transfers between devices  190 us (57%)
  local copies, waits for them, and re-layouts  53.7 us (16%)
  matrix products  35.6 us (11%)
  starting transfers between devices  30.7 us (9%)
  Pallas kernels  16.2 us (5%)
  other arithmetic  5.73 us (2%)
    all_to_all x1, waiting for transfers between devices, shards(): lax.all_to_all(result, 'expert', split_axis=0, concat_axis=0, tiled=True)  86.9 us
    all_to_all x1, waiting for transfers between devices, shards(): lax.all_to_all(packed_two, 'expert', split_axis=0, concat_axis=0, tiled=T...  68.1 us
    all_to_all x1, waiting for transfers between devices, shards(): lax.all_to_all(packed_one, 'expert', split_axis=0, concat_axis=0, tiled=T...  21.5 us
    pallas_call x2, Pallas kernels, attend_normed(): pl.pallas_call(attend_kernel, out_shape=(jax.ShapeDtypeStruct((rows, feat...  16.2 us
    all_to_all x1, waiting for transfers between devices, shards(): lax.all_to_all(result.reshape(received.shape), 'expert', split_axis=0, co...  13.9 us
    dot_general x2, matrix products, expert_rows(): jnp.dot(hidden, down_mat, preferred_element_type=jnp.float32)  13.6 us
    all_to_all x1, starting transfers between devices, shards(): lax.all_to_all(packed_one, 'expert', split_axis=0, concat_axis=0, tiled=T...  12 us
    reshape x2, local copies, waits for them, and re-layouts, shards(): received.reshape(-1, features)  11.3 us
  transfers between devices with their start and end apart: 4, of which 4 were waited for; matrix products, arithmetic and copies ran while one was open for 22% of the time, Pallas kernels for 2%

profile of v3, /device:TPU:8, one launch (start us, length us, event | category | flops | bytes accessed | tf_op | source)
XLA Modules:
  0.0 332.6 jit_solution(1220710870377358436)
XLA Ops:
  11.1 8.1 %shard_map.118 = (f32[64,2560]{1,0:T(8,128)}, bf16[64,2560]{1,0:T(8,128)(2,1)}) custom-call(bf16[64,2560]{1,0:T(8,128)(2,1)} %get-tuple-element.26.query_ref, bf16[64,512]{1,0:T(8,128)(2,1)} %get-tuple-element.39.key_ref, bf16[64,512]{1,0:T(8,128)(2,1)} %get-tuple-element.28.value_ref, s32[1,4]{1,0:T(1,128)} %reduce-window_clone.1.ends_ref, ...), custom_call_target="tpu_custom_call" | custom-call | tf_op jit(solution)/shard_map/pallas_call | solution.py:75
  20.9 3.4 %copy.64 = bf16[64,3,2,2560]{3,2,1,0:T(2,128)(2,1)} copy(bf16[64,3,2,2560]{3,0,2,1:T(8,128)(2,1)S(1)} %convolution_convert_fusion.2) | data formatting | bytes 3932160 | tf_op jit(solution)/shard_map/convert_element_type | solution.py:122
  24.2 12.0 %all-to-all-start = ((bf16[64,3,2,2560]{3,2,1,0:T(2,128)(2,1)}), bf16[64,3,2,2560]{3,2,1,0:T(2,128)(2,1)S(1)}, u32[]{:S(2)}, u32[]{:S(2)}) async-start(bf16[64,3,2,2560]{3,2,1,0:T(2,128)(2,1)} %copy.64), calls=%async_computation | async-start | bytes 3932160 | tf_op jit(solution)/shard_map/all_to_all | solution.py:176
  37.4 8.1 %shard_map.119 = (f32[64,2560]{1,0:T(8,128)}, bf16[64,2560]{1,0:T(8,128)(2,1)}) custom-call(bf16[64,2560]{1,0:T(8,128)(2,1)} %get-tuple-element.27.query_ref, bf16[64,512]{1,0:T(8,128)(2,1)} %get-tuple-element.38.key_ref, bf16[64,512]{1,0:T(8,128)(2,1)} %get-tuple-element.29.value_ref, s32[1,4]{1,0:T(1,128)} %reduce-window_1_clone.1.ends_ref, ...), custom_call_target="tpu_custom_call" | custom-call | tf_op jit(solution)/shard_map/pallas_call | solution.py:75
  46.6 2.9 scatter_custom_fusion
  49.5 4.6 %gather_fusion = bf16[768,2560]{1,0:T(8,128)(2,1)} fusion(bf16[65,2560]{1,0:T(8,128)(2,1)S(1)} %concatenate.3, s32[1024]{0:T(1024)S(1)} %pad_clamp_fusion), kind=kCustom, calls=%fused_computation | custom fusion | bytes 7867392 | tf_op jit(solution)/shard_map/gather | solution.py:132
  54.1 8.7 %reshape.242 = bf16[64,6,2,2560]{3,2,1,0:T(2,128)(2,1)} reshape(bf16[768,2560]{1,0:T(8,128)(2,1)} %gather_fusion) | data formatting | bytes 7864320 | tf_op jit(solution)/shard_map/reshape | solution.py:132
  62.8 21.5 %all-to-all-done = bf16[64,3,2,2560]{3,2,1,0:T(2,128)(2,1)S(1)} async-done(((bf16[64,3,2,2560]{3,2,1,0:T(2,128)(2,1)}), bf16[64,3,2,2560]{3,2,1,0:T(2,128)(2,1)S(1)}, u32[]{:S(2)}, u32[]{:S(2)}) %all-to-all-start) | async-done | bytes 1966112 | tf_op jit(solution)/shard_map/all_to_all | solution.py:176
  84.3 6.6 %all-to-all-start.2 = ((bf16[64,6,2,2560]{3,2,1,0:T(2,128)(2,1)}), bf16[64,6,2,2560]{3,2,1,0:T(2,128)(2,1)}, u32[]{:S(2)}, u32[]{:S(2)}) async-start(bf16[64,6,2,2560]{3,2,1,0:T(2,128)(2,1)} %reshape.242), calls=%async_computation.2 | async-start | bytes 7864320 | tf_op jit(solution)/shard_map/all_to_all | solution.py:191
  90.9 2.2 reshape.238
  93.2 4.5 %fusion.8 = f32[384,768]{1,0:T(8,128)S(1)} fusion(bf16[384,2560]{1,0:T(8,128)(2,1)} %reshape.238, bf16[1,2560,768]{2,1,0:T(8,128)(2,1)} %param.21), kind=kOutput, calls=%fused_computation.13 | convolution fusion | flops 1509949440 | bytes 7077888 | tf_op jit(solution)/shard_map/dot_general | solution.py:92
  97.7 8.8 %convolution_convert_fusion.1 = bf16[384,2560]{1,0:T(8,128)(2,1)} fusion(bf16[1,768,2560]{2,1,0:T(8,128)(2,1)} %param.23, bf16[384,2560]{1,0:T(8,128)(2,1)S(1)} %copy-done.1, bf16[1,2560,768]{2,1,0:T(8,128)(2,1)} %param.22, f32[384,768]{1,0:T(8,128)S(1)} %fusion.8), kind=kOutput, calls=%fused_computation.3 | convolution fusion | flops 3022651392 | bytes 12976128 | tf_op jit(solution)/shard_map/dot_general | solution.py:95
  106.5 5.0 %reshape.239 = bf16[64,3,2,2560]{3,2,1,0:T(2,128)(2,1)} reshape(bf16[384,2560]{1,0:T(8,128)(2,1)} %convolution_convert_fusion.1) | data formatting | bytes 3932160 | tf_op jit(solution)/shard_map/reshape | solution.py:185
  111.5 68.1 %all-to-all-done.2 = bf16[64,6,2,2560]{3,2,1,0:T(2,128)(2,1)} async-done(((bf16[64,6,2,2560]{3,2,1,0:T(2,128)(2,1)}), bf16[64,6,2,2560]{3,2,1,0:T(2,128)(2,1)}, u32[]{:S(2)}, u32[]{:S(2)}) %all-to-all-start.2) | async-done | bytes 3932192 | tf_op jit(solution)/shard_map/all_to_all | solution.py:191
  179.7 5.7 %all-to-all-start.1 = ((bf16[64,3,2,2560]{3,2,1,0:T(2,128)(2,1)}), bf16[64,3,2,2560]{3,2,1,0:T(2,128)(2,1)S(1)}, u32[]{:S(2)}, u32[]{:S(2)}) async-start(bf16[64,3,2,2560]{3,2,1,0:T(2,128)(2,1)} %reshape.239), calls=%async_computation.1 | async-start | bytes 3932160 | tf_op jit(solution)/shard_map/all_to_all | solution.py:184
  185.3 9.1 %reshape.243 = bf16[768,2560]{1,0:T(8,128)(2,1)} reshape(bf16[64,6,2,2560]{3,2,1,0:T(2,128)(2,1)} %all-to-all-done.2) | data formatting | bytes 7864320 | tf_op jit(solution)/shard_map/reshape | solution.py:198
  194.4 6.6 %fusion.2 = f32[768,768]{1,0:T(8,128)S(1)} fusion(bf16[768,2560]{1,0:T(8,128)(2,1)} %reshape.243, bf16[1,2560,768]{2,1,0:T(8,128)(2,1)} %param.22), kind=kOutput, calls=%fused_computation.7 | convolution fusion | flops 3019898880 | bytes 10223616 | tf_op jit(solution)/shard_map/dot_general | solution.py:93
  201.1 3.4 %multiply_convert_fusion = bf16[768,768]{1,0:T(8,128)(2,1)S(1)} fusion(f32[768,768]{1,0:T(8,128)S(1)} %fusion.2, bf16[768,2560]{1,0:T(8,128)(2,1)S(1)} %copy-done, bf16[1,2560,768]{2,1,0:T(8,128)(2,1)S(1)} %copy-done.3), kind=kOutput, calls=%fused_computation.25 | convolution fusion | flops 3023437824 | bytes 11403264 | tf_op jit(solution)/shard_map/dot_general | solution.py:92
  204.5 4.8 %convolution_convert_fusion = bf16[768,2560]{1,0:T(8,128)(2,1)} fusion(bf16[768,768]{1,0:T(8,128)(2,1)S(1)} %multiply_convert_fusion, bf16[1,768,2560]{2,1,0:T(8,128)(2,1)S(1)} %copy-done.4), kind=kOutput, calls=%fused_computation.2 | convolution fusion | flops 3021864960 | bytes 9043968 | tf_op jit(solution)/shard_map/dot_general | solution.py:95
  209.3 8.7 %reshape.244 = bf16[64,6,2,2560]{3,2,1,0:T(2,128)(2,1)} reshape(bf16[768,2560]{1,0:T(8,128)(2,1)} %convolution_convert_fusion) | data formatting | bytes 7864320 | tf_op jit(solution)/shard_map/reshape | solution.py:198
  218.0 13.9 %all-to-all-done.1 = bf16[64,3,2,2560]{3,2,1,0:T(2,128)(2,1)S(1)} async-done(((bf16[64,3,2,2560]{3,2,1,0:T(2,128)(2,1)}), bf16[64,3,2,2560]{3,2,1,0:T(2,128)(2,1)S(1)}, u32[]{:S(2)}, u32[]{:S(2)}) %all-to-all-start.1) | async-done | bytes 1966112 | tf_op jit(solution)/shard_map/all_to_all | solution.py:184
  231.9 6.4 %all-to-all-start.3 = ((bf16[64,6,2,2560]{3,2,1,0:T(2,128)(2,1)}), bf16[64,6,2,2560]{3,2,1,0:T(2,128)(2,1)}, u32[]{:S(2)}, u32[]{:S(2)}) async-start(bf16[64,6,2,2560]{3,2,1,0:T(2,128)(2,1)} %reshape.244), calls=%async_computation.3 | async-start | bytes 7864320 | tf_op jit(solution)/shard_map/all_to_all | solution.py:201
  240.2 86.9 %all-to-all-done.3 = bf16[64,6,2,2560]{3,2,1,0:T(2,128)(2,1)} async-done(((bf16[64,6,2,2560]{3,2,1,0:T(2,128)(2,1)}), bf16[64,6,2,2560]{3,2,1,0:T(2,128)(2,1)}, u32[]{:S(2)}, u32[]{:S(2)}) %all-to-all-start.3) | async-done | bytes 3932192 | tf_op jit(solution)/shard_map/all_to_all | solution.py:201
  327.1 4.6 %fusion.24 = bf16[1,64,2560]{2,1,0:T(8,128)(2,1)S(1)} fusion(f32[64,2560]{1,0:T(8,128)} %get-tuple-element.11, bf16[64,6,2,2560]{3,2,1,0:T(2,128)(2,1)} %all-to-all-done.3, f32[64,64,6,2]{0,3,2,1:T(2,128)S(1)} %bitcast.109), kind=kOutput, calls=%fused_computation.24 | convolution fusion | flops 1510277120 | bytes 5111808 | tf_op jit(solution)/shard_map/tabc,abcf->tf/dot_general | solution.py:140
  (51 shorter events, 17.6 us)
Async XLA Ops:
  24.2 60.1 %all-to-all-start = ((bf16[64,3,2,2560]{3,2,1,0:T(2,128)(2,1)}), bf16[64,3,2,2560]{3,2,1,0:T(2,128)(2,1)S(1)}, u32[]{:S(2)}, u32[]{:S(2)}) async-start(bf16[64,3,2,2560]{3,2,1,0:T(2,128)(2,1)} %copy.64), calls=%async_computation | async-start | bytes 3932160 | tf_op jit(solution)/shard_map/all_to_all | solution.py:176
  84.3 95.4 %all-to-all-start.2 = ((bf16[64,6,2,2560]{3,2,1,0:T(2,128)(2,1)}), bf16[64,6,2,2560]{3,2,1,0:T(2,128)(2,1)}, u32[]{:S(2)}, u32[]{:S(2)}) async-start(bf16[64,6,2,2560]{3,2,1,0:T(2,128)(2,1)} %reshape.242), calls=%async_computation.2 | async-start | bytes 7864320 | tf_op jit(solution)/shard_map/all_to_all | solution.py:191
  93.2 4.5 %copy-start.1 = (bf16[384,2560]{1,0:T(8,128)(2,1)S(1)}, bf16[384,2560]{1,0:T(8,128)(2,1)}, u32[]{:S(2)}) copy-start(bf16[384,2560]{1,0:T(8,128)(2,1)} %reshape.238) | copy-start | bytes 5898244
  179.7 52.2 %all-to-all-start.1 = ((bf16[64,3,2,2560]{3,2,1,0:T(2,128)(2,1)}), bf16[64,3,2,2560]{3,2,1,0:T(2,128)(2,1)S(1)}, u32[]{:S(2)}, u32[]{:S(2)}) async-start(bf16[64,3,2,2560]{3,2,1,0:T(2,128)(2,1)} %reshape.239), calls=%async_computation.1 | async-start | bytes 3932160 | tf_op jit(solution)/shard_map/all_to_all | solution.py:184
  194.4 6.7 %copy-start = (bf16[768,2560]{1,0:T(8,128)(2,1)S(1)}, bf16[768,2560]{1,0:T(8,128)(2,1)}, u32[]{:S(2)}) copy-start(bf16[768,2560]{1,0:T(8,128)(2,1)} %reshape.243) | copy-start | bytes 11796484
  194.4 6.7 %copy-start.3 = (bf16[1,2560,768]{2,1,0:T(8,128)(2,1)S(1)}, bf16[1,2560,768]{2,1,0:T(8,128)(2,1)}, u32[]{:S(2)}) copy-start(bf16[1,2560,768]{2,1,0:T(8,128)(2,1)} %param.21) | copy-start | bytes 11796484
  201.1 3.5 %copy-start.4 = (bf16[1,768,2560]{2,1,0:T(8,128)(2,1)S(1)}, bf16[1,768,2560]{2,1,0:T(8,128)(2,1)}, u32[]{:S(2)}) copy-start(bf16[1,768,2560]{2,1,0:T(8,128)(2,1)} %param.23) | copy-start | bytes 11796484
  218.0 21.0 %copy-start.2 = (f32[64,2560]{1,0:T(8,128)S(1)}, f32[64,2560]{1,0:T(8,128)}, u32[]{:S(2)}) copy-start(f32[64,2560]{1,0:T(8,128)} %get-tuple-element.9) | copy-start | bytes 1966084
  231.9 95.2 %all-to-all-start.3 = ((bf16[64,6,2,2560]{3,2,1,0:T(2,128)(2,1)}), bf16[64,6,2,2560]{3,2,1,0:T(2,128)(2,1)}, u32[]{:S(2)}, u32[]{:S(2)}) async-start(bf16[64,6,2,2560]{3,2,1,0:T(2,128)(2,1)} %reshape.244), calls=%async_computation.3 | async-start | bytes 7864320 | tf_op jit(solution)/shard_map/all_to_all | solution.py:201

commit v4 on v3

--- a/solution.py
+++ b/solution.py
@@ -34,12 +34,10 @@
 def attend_kernel(query_ref, key_ref, value_ref, ends_ref, gain_ref, attn_ref, normed_ref):
     rows = query_ref.shape[0]
     kv_heads = key_ref.shape[1] // HEAD_WIDTH
-    query_group = query_ref.shape[1] // HEAD_WIDTH // kv_heads
+    group = query_ref.shape[1] // HEAD_WIDTH // kv_heads
     ends = ends_ref[...]
     position = lax.broadcasted_iota(jnp.int32, (rows, ends.shape[1]), 0)
     request = jnp.sum((position >= ends).astype(jnp.int32), axis=1, keepdims=True)
-    row = lax.broadcasted_iota(jnp.int32, (rows, rows), 0)
-    col = lax.broadcasted_iota(jnp.int32, (rows, rows), 1)
     request_col = jnp.sum(
         (lax.broadcasted_iota(jnp.int32, (ends.shape[1], rows), 1) >= ends.reshape(-1, 1)).astype(
             jnp.int32
@@ -47,10 +45,18 @@
         axis=0,
         keepdims=True,
     )
+    row = lax.broadcasted_iota(jnp.int32, (rows, rows), 0)
+    col = lax.broadcasted_iota(jnp.int32, (rows, rows), 1)
     allowed = (request == request_col) & (col <= row)
-    for head in range(kv_heads * query_group):
-        kv = head // query_group
-        q = query_ref[:, head * HEAD_WIDTH : (head + 1) * HEAD_WIDTH]
+    allowed = jnp.concatenate([allowed] * group, axis=0)
+    for kv in range(kv_heads):
+        q = jnp.concatenate(
+            [
+                query_ref[:, (kv * group + g) * HEAD_WIDTH : (kv * group + g + 1) * HEAD_WIDTH]
+                for g in range(group)
+            ],
+            axis=0,
+        )
         k = key_ref[:, kv * HEAD_WIDTH : (kv + 1) * HEAD_WIDTH]
         v = value_ref[:, kv * HEAD_WIDTH : (kv + 1) * HEAD_WIDTH]
         logits = lax.dot_general(
@@ -60,26 +66,40 @@
         highest = jnp.max(logits, axis=-1, keepdims=True)
         weights = jnp.exp(logits - highest)
         probs = (weights / jnp.sum(weights, axis=-1, keepdims=True)).astype(jnp.bfloat16)
-        attn_ref[:, head * HEAD_WIDTH : (head + 1) * HEAD_WIDTH] = jnp.dot(
-            probs, v, preferred_element_type=jnp.float32
-        )
+        mixed = jnp.dot(probs, v, preferred_element_type=jnp.float32)
+        for g in range(group):
+            head = kv * group + g
+            attn_ref[:, head * HEAD_WIDTH : (head + 1) * HEAD_WIDTH] = mixed[g * rows : (g + 1) * rows]
     attn = attn_ref[...]
     meansq = jnp.mean(attn * attn, axis=-1, keepdims=True)
     normed_ref[...] = (attn * lax.rsqrt(meansq + 1e-05) * gain_ref[...]).astype(jnp.bfloat16)
 
 
-def attend_normed(query, key_rows, value_rows, lengths, gain):
-    rows, features = query.shape
-    ends = jnp.cumsum(lengths).reshape(1, -1)
-    vmem = pl.BlockSpec(memory_space=pltpu.VMEM)
+def attend_normed(batch, query, key_rows, value_rows, lengths, gain):
+    rows, features = query.shape[1:]
+    ends = jnp.cumsum(lengths, axis=-1)
+
+    def pick(array):
+        return pl.BlockSpec((None,) + array.shape[1:], lambda i: (batch, 0, 0))
+
     return pl.pallas_call(
         attend_kernel,
+        grid=(1,),
         out_shape=(
             jax.ShapeDtypeStruct((rows, features), jnp.float32),
             jax.ShapeDtypeStruct((rows, features), jnp.bfloat16),
         ),
-        in_specs=[vmem] * 5,
-        out_specs=(vmem, vmem),
+        in_specs=[
+            pick(query),
+            pick(key_rows),
+            pick(value_rows),
+            pick(ends),
+            pl.BlockSpec((1, features), lambda i: (0, 0)),
+        ],
+        out_specs=(
+            pl.BlockSpec((rows, features), lambda i: (0, 0)),
+            pl.BlockSpec((rows, features), lambda i: (0, 0)),
+        ),
     )(query, key_rows, value_rows, ends, gain.reshape(1, -1))
 
 
@@ -170,7 +190,7 @@
     )
     doubled = jnp.sum((dup_experts[:, None] == expert_list[None, :]).astype(jnp.int32), axis=0)
     own_gate, own_up, own_down = (w_gate[0], w_up[0], w_down[0])
-    attn_one, normed_one = attend_normed(query[0], keys[0], values[0], lengths[0, 0], norm_gain)
+    attn_one, normed_one = attend_normed(0, query, keys, values, lengths, norm_gain)
     flat_one, kept_one = routing(routes[0], jnp.ones_like(doubled), holder, holder, 1)
     packed_one, spot_one = pack(normed_one, flat_one, kept_one, (width, CAP // 2, 2))
     received = lax.all_to_all(
@@ -185,7 +205,7 @@
         result.reshape(received.shape), "expert", split_axis=0, concat_axis=0, tiled=True
     )
     out_one = combine(attn_one, back_one, spot_one, kept_one, gates[0])
-    attn_two, normed_two = attend_normed(query[1], keys[1], values[1], lengths[1, 0], norm_gain)
+    attn_two, normed_two = attend_normed(1, query, keys, values, lengths, norm_gain)
     flat_two, kept_two = routing(routes[1], 1 + doubled, holder, holder, 2)
     packed_two, spot_two = gather_pack(normed_two, flat_two, kept_two, (width, CAP, 2))
     received = lax.all_to_all(

time: 334 us -> 325 us (0.973)
  Pallas kernels: 16.2 us -> 5.78 us
  waiting for transfers between devices: 190 us -> 195 us
  local copies, waits for them, and re-layouts: 53.7 us -> 49.3 us
    pallas_call x2, Pallas kernels: 16.2 us -> 5.78 us  [attend_normed(): pl.pallas_call(attend_kernel, grid=(1,), out_shape=(jax.ShapeDtypeStruct(...]
    all_to_all x1, waiting for transfers between devices: 21.5 us -> 27.5 us  [shards(): lax.all_to_all(packed_one, 'expert', split_axis=0, concat_axis=0, tiled=T...]
    squeeze x2 -> x0, local copies, waits for them, and re-layouts: 3.61 us -> none  [the longest x1 1.95 us: shards(): query[0]]
  transfers between devices with their start and end apart: 4 -> 4, of which waited for: 4 -> 4; matrix products, arithmetic and copies ran while one was open for 22% -> 23% of each run, Pallas kernels for 2% -> 1%
where the time goes in v4:
time: 325 us; the launch traced here: 324 us
  waiting for transfers between devices  195 us (60%)
  local copies, waits for them, and re-layouts  49.3 us (15%)
  matrix products  37.1 us (11%)
  starting transfers between devices  30.6 us (9%)
  Pallas kernels  5.78 us (2%)
  other arithmetic  5.71 us (2%)
    all_to_all x1, waiting for transfers between devices, shards(): lax.all_to_all(result, 'expert', split_axis=0, concat_axis=0, tiled=True)  86.9 us
    all_to_all x1, waiting for transfers between devices, shards(): lax.all_to_all(packed_two, 'expert', split_axis=0, concat_axis=0, tiled=T...  66.7 us
    all_to_all x1, waiting for transfers between devices, shards(): lax.all_to_all(packed_one, 'expert', split_axis=0, concat_axis=0, tiled=T...  27.5 us
    dot_general x2, matrix products, expert_rows(): jnp.dot(hidden, down_mat, preferred_element_type=jnp.float32)  13.9 us
    all_to_all x1, waiting for transfers between devices, shards(): lax.all_to_all(result.reshape(received.shape), 'expert', split_axis=0, co...  13.9 us
    all_to_all x1, starting transfers between devices, shards(): lax.all_to_all(packed_one, 'expert', split_axis=0, concat_axis=0, tiled=T...  12 us
    reshape x2, local copies, waits for them, and re-layouts, shards(): received.reshape(-1, features)  11.3 us
    dot_general x2, matrix products, expert_rows(): gate_val = jnp.dot(rows, gate_mat, preferred_element_type=jnp.float32)  9.06 us
  transfers between devices with their start and end apart: 4, of which 4 were waited for; matrix products, arithmetic and copies ran while one was open for 23% of the time, Pallas kernels for 1%

profile of v4, /device:TPU:8, one launch (start us, length us, event | category | flops | bytes accessed | tf_op | source)
XLA Modules:
  0.0 323.6 jit_solution(11642155573797478171)
XLA Ops:
  7.6 2.9 shard_map.118
  12.1 3.3 %copy.64 = bf16[64,3,2,2560]{3,2,1,0:T(2,128)(2,1)} copy(bf16[64,3,2,2560]{3,0,2,1:T(8,128)(2,1)S(1)} %convolution_convert_fusion.2) | data formatting | bytes 3932160 | tf_op jit(solution)/shard_map/convert_element_type | solution.py:142
  15.4 12.0 %all-to-all-start = ((bf16[64,3,2,2560]{3,2,1,0:T(2,128)(2,1)}), bf16[64,3,2,2560]{3,2,1,0:T(2,128)(2,1)S(1)}, u32[]{:S(2)}, u32[]{:S(2)}) async-start(bf16[64,3,2,2560]{3,2,1,0:T(2,128)(2,1)} %copy.64), calls=%async_computation | async-start | bytes 3932160 | tf_op jit(solution)/shard_map/all_to_all | solution.py:196
  27.4 2.9 shard_map.119
  31.7 2.9 scatter_custom_fusion
  34.7 4.5 %gather_fusion = bf16[768,2560]{1,0:T(8,128)(2,1)} fusion(bf16[65,2560]{1,0:T(8,128)(2,1)S(1)} %concatenate.3, s32[1024]{0:T(1024)S(1)} %pad_clamp_fusion), kind=kCustom, calls=%fused_computation | custom fusion | bytes 7867392 | tf_op jit(solution)/shard_map/gather | solution.py:152
  39.2 8.7 %reshape.222 = bf16[64,6,2,2560]{3,2,1,0:T(2,128)(2,1)} reshape(bf16[768,2560]{1,0:T(8,128)(2,1)} %gather_fusion) | data formatting | bytes 7864320 | tf_op jit(solution)/shard_map/reshape | solution.py:152
  48.0 27.5 %all-to-all-done = bf16[64,3,2,2560]{3,2,1,0:T(2,128)(2,1)S(1)} async-done(((bf16[64,3,2,2560]{3,2,1,0:T(2,128)(2,1)}), bf16[64,3,2,2560]{3,2,1,0:T(2,128)(2,1)S(1)}, u32[]{:S(2)}, u32[]{:S(2)}) %all-to-all-start) | async-done | bytes 1966112 | tf_op jit(solution)/shard_map/all_to_all | solution.py:196
  75.5 6.5 %all-to-all-start.2 = ((bf16[64,6,2,2560]{3,2,1,0:T(2,128)(2,1)}), bf16[64,6,2,2560]{3,2,1,0:T(2,128)(2,1)}, u32[]{:S(2)}, u32[]{:S(2)}) async-start(bf16[64,6,2,2560]{3,2,1,0:T(2,128)(2,1)} %reshape.222), calls=%async_computation.2 | async-start | bytes 7864320 | tf_op jit(solution)/shard_map/all_to_all | solution.py:211
  81.9 2.2 reshape.219
  84.2 5.6 %fusion.8 = f32[384,768]{1,0:T(8,128)} fusion(bf16[384,2560]{1,0:T(8,128)(2,1)} %reshape.219, bf16[1,2560,768]{2,1,0:T(8,128)(2,1)} %param.21), kind=kOutput, calls=%fused_computation.13 | convolution fusion | flops 1509949440 | bytes 7077888 | tf_op jit(solution)/shard_map/dot_general | solution.py:112
  89.8 9.2 %convolution_convert_fusion.1 = bf16[384,2560]{1,0:T(8,128)(2,1)} fusion(bf16[1,768,2560]{2,1,0:T(8,128)(2,1)} %param.23, bf16[384,2560]{1,0:T(8,128)(2,1)S(1)} %copy-done.1, bf16[1,2560,768]{2,1,0:T(8,128)(2,1)} %param.22, f32[384,768]{1,0:T(8,128)} %fusion.8), kind=kOutput, calls=%fused_computation.3 | convolution fusion | flops 3022651392 | bytes 12976128 | tf_op jit(solution)/shard_map/dot_general | solution.py:115
  99.0 5.0 %reshape.220 = bf16[64,3,2,2560]{3,2,1,0:T(2,128)(2,1)} reshape(bf16[384,2560]{1,0:T(8,128)(2,1)} %convolution_convert_fusion.1) | data formatting | bytes 3932160 | tf_op jit(solution)/shard_map/reshape | solution.py:205
  104.0 66.7 %all-to-all-done.2 = bf16[64,6,2,2560]{3,2,1,0:T(2,128)(2,1)} async-done(((bf16[64,6,2,2560]{3,2,1,0:T(2,128)(2,1)}), bf16[64,6,2,2560]{3,2,1,0:T(2,128)(2,1)}, u32[]{:S(2)}, u32[]{:S(2)}) %all-to-all-start.2) | async-done | bytes 3932192 | tf_op jit(solution)/shard_map/all_to_all | solution.py:211
  170.7 5.7 %all-to-all-start.1 = ((bf16[64,3,2,2560]{3,2,1,0:T(2,128)(2,1)}), bf16[64,3,2,2560]{3,2,1,0:T(2,128)(2,1)S(1)}, u32[]{:S(2)}, u32[]{:S(2)}) async-start(bf16[64,3,2,2560]{3,2,1,0:T(2,128)(2,1)} %reshape.220), calls=%async_computation.1 | async-start | bytes 3932160 | tf_op jit(solution)/shard_map/all_to_all | solution.py:204
  176.4 9.0 %reshape.223 = bf16[768,2560]{1,0:T(8,128)(2,1)} reshape(bf16[64,6,2,2560]{3,2,1,0:T(2,128)(2,1)} %all-to-all-done.2) | data formatting | bytes 7864320 | tf_op jit(solution)/shard_map/reshape | solution.py:218
  185.4 6.6 %fusion.2 = f32[768,768]{1,0:T(8,128)S(1)} fusion(bf16[768,2560]{1,0:T(8,128)(2,1)} %reshape.223, bf16[1,2560,768]{2,1,0:T(8,128)(2,1)} %param.22), kind=kOutput, calls=%fused_computation.7 | convolution fusion | flops 3019898880 | bytes 10223616 | tf_op jit(solution)/shard_map/dot_general | solution.py:113
  192.1 3.4 %multiply_convert_fusion = bf16[768,768]{1,0:T(8,128)(2,1)S(1)} fusion(f32[768,768]{1,0:T(8,128)S(1)} %fusion.2, bf16[768,2560]{1,0:T(8,128)(2,1)S(1)} %copy-done, bf16[1,2560,768]{2,1,0:T(8,128)(2,1)S(1)} %copy-done.3), kind=kOutput, calls=%fused_computation.25 | convolution fusion | flops 3023437824 | bytes 11403264 | tf_op jit(solution)/shard_map/dot_general | solution.py:112
  195.5 4.8 %convolution_convert_fusion = bf16[768,2560]{1,0:T(8,128)(2,1)} fusion(bf16[768,768]{1,0:T(8,128)(2,1)S(1)} %multiply_convert_fusion, bf16[1,768,2560]{2,1,0:T(8,128)(2,1)S(1)} %copy-done.4), kind=kOutput, calls=%fused_computation.2 | convolution fusion | flops 3021864960 | bytes 9043968 | tf_op jit(solution)/shard_map/dot_general | solution.py:115
  200.3 8.7 %reshape.224 = bf16[64,6,2,2560]{3,2,1,0:T(2,128)(2,1)} reshape(bf16[768,2560]{1,0:T(8,128)(2,1)} %convolution_convert_fusion) | data formatting | bytes 7864320 | tf_op jit(solution)/shard_map/reshape | solution.py:218
  209.0 13.9 %all-to-all-done.1 = bf16[64,3,2,2560]{3,2,1,0:T(2,128)(2,1)S(1)} async-done(((bf16[64,3,2,2560]{3,2,1,0:T(2,128)(2,1)}), bf16[64,3,2,2560]{3,2,1,0:T(2,128)(2,1)S(1)}, u32[]{:S(2)}, u32[]{:S(2)}) %all-to-all-start.1) | async-done | bytes 1966112 | tf_op jit(solution)/shard_map/all_to_all | solution.py:204
  222.9 6.5 %all-to-all-start.3 = ((bf16[64,6,2,2560]{3,2,1,0:T(2,128)(2,1)}), bf16[64,6,2,2560]{3,2,1,0:T(2,128)(2,1)}, u32[]{:S(2)}, u32[]{:S(2)}) async-start(bf16[64,6,2,2560]{3,2,1,0:T(2,128)(2,1)} %reshape.224), calls=%async_computation.3 | async-start | bytes 7864320 | tf_op jit(solution)/shard_map/all_to_all | solution.py:221
  231.2 86.9 %all-to-all-done.3 = bf16[64,6,2,2560]{3,2,1,0:T(2,128)(2,1)} async-done(((bf16[64,6,2,2560]{3,2,1,0:T(2,128)(2,1)}), bf16[64,6,2,2560]{3,2,1,0:T(2,128)(2,1)}, u32[]{:S(2)}, u32[]{:S(2)}) %all-to-all-start.3) | async-done | bytes 3932192 | tf_op jit(solution)/shard_map/all_to_all | solution.py:221
  318.1 4.6 %fusion.24 = bf16[1,64,2560]{2,1,0:T(8,128)(2,1)S(1)} fusion(f32[64,2560]{1,0:T(8,128)} %get-tuple-element.11, bf16[64,6,2,2560]{3,2,1,0:T(2,128)(2,1)} %all-to-all-done.3, f32[64,64,6,2]{0,3,2,1:T(2,128)S(1)} %bitcast.93), kind=kOutput, calls=%fused_computation.24 | convolution fusion | flops 1510277120 | bytes 5111808 | tf_op jit(solution)/shard_map/tabc,abcf->tf/dot_general | solution.py:160
  (47 shorter events, 13.3 us)
Async XLA Ops:
  15.4 60.1 %all-to-all-start = ((bf16[64,3,2,2560]{3,2,1,0:T(2,128)(2,1)}), bf16[64,3,2,2560]{3,2,1,0:T(2,128)(2,1)S(1)}, u32[]{:S(2)}, u32[]{:S(2)}) async-start(bf16[64,3,2,2560]{3,2,1,0:T(2,128)(2,1)} %copy.64), calls=%async_computation | async-start | bytes 3932160 | tf_op jit(solution)/shard_map/all_to_all | solution.py:196
  75.5 95.2 %all-to-all-start.2 = ((bf16[64,6,2,2560]{3,2,1,0:T(2,128)(2,1)}), bf16[64,6,2,2560]{3,2,1,0:T(2,128)(2,1)}, u32[]{:S(2)}, u32[]{:S(2)}) async-start(bf16[64,6,2,2560]{3,2,1,0:T(2,128)(2,1)} %reshape.222), calls=%async_computation.2 | async-start | bytes 7864320 | tf_op jit(solution)/shard_map/all_to_all | solution.py:211
  84.2 5.6 %copy-start.1 = (bf16[384,2560]{1,0:T(8,128)(2,1)S(1)}, bf16[384,2560]{1,0:T(8,128)(2,1)}, u32[]{:S(2)}) copy-start(bf16[384,2560]{1,0:T(8,128)(2,1)} %reshape.219) | copy-start | bytes 5898244
  170.7 52.2 %all-to-all-start.1 = ((bf16[64,3,2,2560]{3,2,1,0:T(2,128)(2,1)}), bf16[64,3,2,2560]{3,2,1,0:T(2,128)(2,1)S(1)}, u32[]{:S(2)}, u32[]{:S(2)}) async-start(bf16[64,3,2,2560]{3,2,1,0:T(2,128)(2,1)} %reshape.220), calls=%async_computation.1 | async-start | bytes 3932160 | tf_op jit(solution)/shard_map/all_to_all | solution.py:204
  185.4 6.7 %copy-start = (bf16[768,2560]{1,0:T(8,128)(2,1)S(1)}, bf16[768,2560]{1,0:T(8,128)(2,1)}, u32[]{:S(2)}) copy-start(bf16[768,2560]{1,0:T(8,128)(2,1)} %reshape.223) | copy-start | bytes 11796484
  185.4 6.7 %copy-start.3 = (bf16[1,2560,768]{2,1,0:T(8,128)(2,1)S(1)}, bf16[1,2560,768]{2,1,0:T(8,128)(2,1)}, u32[]{:S(2)}) copy-start(bf16[1,2560,768]{2,1,0:T(8,128)(2,1)} %param.21) | copy-start | bytes 11796484
  192.1 3.5 %copy-start.4 = (bf16[1,768,2560]{2,1,0:T(8,128)(2,1)S(1)}, bf16[1,768,2560]{2,1,0:T(8,128)(2,1)}, u32[]{:S(2)}) copy-start(bf16[1,768,2560]{2,1,0:T(8,128)(2,1)} %param.23) | copy-start | bytes 11796484
  209.0 21.0 %copy-start.2 = (f32[64,2560]{1,0:T(8,128)S(1)}, f32[64,2560]{1,0:T(8,128)}, u32[]{:S(2)}) copy-start(f32[64,2560]{1,0:T(8,128)} %get-tuple-element.9) | copy-start | bytes 1966084
  222.9 95.2 %all-to-all-start.3 = ((bf16[64,6,2,2560]{3,2,1,0:T(2,128)(2,1)}), bf16[64,6,2,2560]{3,2,1,0:T(2,128)(2,1)}, u32[]{:S(2)}, u32[]{:S(2)}) async-start(bf16[64,6,2,2560]{3,2,1,0:T(2,128)(2,1)} %reshape.224), calls=%async_computation.3 | async-start | bytes 7864320 | tf_op jit(solution)/shard_map/all_to_all | solution.py:221

commit v5 on v0

--- a/solution.py
+++ b/solution.py
@@ -78,18 +78,27 @@
     return (padded[source_row].reshape(shape + (normed.shape[1],)), spot)
 
 
-def combine(attn, returned, spot, kept, gates):
+def combine(attn, returned, spot, kept, gates, split=False):
     slots = returned.size // returned.shape[-1]
     weight = jnp.where(kept, gates, 0.0)
     onehot = (spot[:, :, None] == lax.iota(jnp.int32, slots)[None, None, :]).astype(jnp.float32)
     spread = jnp.sum(onehot * weight[:, :, None], axis=1).reshape((-1,) + returned.shape[:-1])
-    mixed = jnp.einsum(
-        "tabc,abcf->tf",
-        spread,
-        returned.astype(jnp.float32),
-        precision=lax.Precision.HIGHEST,
-        preferred_element_type=jnp.float32,
-    )
+    if split:
+        high = spread.astype(returned.dtype)
+        rest = spread - high.astype(jnp.float32)
+        middle = rest.astype(returned.dtype)
+        mixed = sum(
+            jnp.einsum("tabc,abcf->tf", part, returned, preferred_element_type=jnp.float32)
+            for part in (high, middle)
+        )
+    else:
+        mixed = jnp.einsum(
+            "tabc,abcf->tf",
+            spread,
+            returned.astype(jnp.float32),
+            precision=lax.Precision.HIGHEST,
+            preferred_element_type=jnp.float32,
+        )
     return (attn + mixed).astype(jnp.bfloat16)
 
 
@@ -147,7 +156,7 @@
         received.shape
     )
     back_two = lax.all_to_all(result, "expert", split_axis=0, concat_axis=0, tiled=True)
-    out_two = combine(attn_two, back_two, spot_two, kept_two, gates[1])
+    out_two = combine(attn_two, back_two, spot_two, kept_two, gates[1], split=True)
     return jnp.stack([out_one, out_two])
 
 

time: 320 us -> 322 us (level)
    dot_general x0 -> x2, matrix products: none -> 5.97 us  [combine(): jnp.einsum('tabc,abcf->tf', part, returned, preferred_element_type=jnp.fl...]
    dot_general x2 -> x1, matrix products: 6.86 us -> 2.39 us  [combine(): jnp.einsum('tabc,abcf->tf', spread, returned.astype(jnp.float32), precisi...]
where the time goes in v5:
time: 322 us; the launch traced here: 321 us
  waiting for transfers between devices  186 us (58%)
  local copies, waits for them, and re-layouts  58.1 us (18%)
  matrix products  41.3 us (13%)
  starting transfers between devices  30.6 us (10%)
  other arithmetic  4.86 us (2%)
    all_to_all x1, waiting for transfers between devices, shards(): lax.all_to_all(result, 'expert', split_axis=0, concat_axis=0, tiled=True)  79.2 us
    all_to_all x1, waiting for transfers between devices, shards(): lax.all_to_all(packed_two, 'expert', split_axis=0, concat_axis=0, tiled=T...  66.6 us
    all_to_all x1, waiting for transfers between devices, shards(): lax.all_to_all(packed_one, 'expert', split_axis=0, concat_axis=0, tiled=T...  26 us
    dot_general x2, matrix products, expert_rows(): jnp.dot(hidden, down_mat, preferred_element_type=jnp.float32)  14 us
    all_to_all x1, waiting for transfers between devices, shards(): lax.all_to_all(result.reshape(received.shape), 'expert', split_axis=0, co...  13.9 us
    all_to_all x1, starting transfers between devices, shards(): lax.all_to_all(packed_one, 'expert', split_axis=0, concat_axis=0, tiled=T...  12 us
    reshape x2, local copies, waits for them, and re-layouts, shards(): received.reshape(-1, features)  11.3 us
    dot_general x2, matrix products, expert_rows(): gate_val = jnp.dot(rows, gate_mat, preferred_element_type=jnp.float32)  9.09 us
  transfers between devices with their start and end apart: 4, of which 4 were waited for; matrix products, arithmetic and copies ran while one was open for 27% of the time, Pallas kernels for 0%

profile of v5, /device:TPU:8, one launch (start us, length us, event | category | flops | bytes accessed | tf_op | source)
XLA Modules:
  0.0 321.0 jit_solution(13638836612975630145)
XLA Ops:
  8.1 3.3 %copy.98 = bf16[64,3,2,2560]{3,2,1,0:T(2,128)(2,1)} copy(bf16[64,3,2,2560]{3,0,2,1:T(8,128)(2,1)S(1)} %convolution_convert_fusion.2) | data formatting | bytes 3932160 | tf_op jit(solution)/shard_map/convert_element_type | solution.py:68
  11.5 12.0 %all-to-all-start = ((bf16[64,3,2,2560]{3,2,1,0:T(2,128)(2,1)}), bf16[64,3,2,2560]{3,2,1,0:T(2,128)(2,1)S(1)}, u32[]{:S(2)}, u32[]{:S(2)}) async-start(bf16[64,3,2,2560]{3,2,1,0:T(2,128)(2,1)} %copy.98), calls=%async_computation | async-start | bytes 3932160 | tf_op jit(solution)/shard_map/all_to_all | solution.py:132
  29.0 3.1 scatter_custom_fusion
  32.2 4.6 %gather_fusion = bf16[768,2560]{1,0:T(8,128)(2,1)} fusion(bf16[65,2560]{1,0:T(8,128)(2,1)S(1)} %concatenate.3, s32[1024]{0:T(1024)S(1)} %pad_clamp_fusion), kind=kCustom, calls=%fused_computation | custom fusion | bytes 7867392 | tf_op jit(solution)/shard_map/gather | solution.py:78
  36.8 8.7 %reshape.388 = bf16[64,6,2,2560]{3,2,1,0:T(2,128)(2,1)} reshape(bf16[768,2560]{1,0:T(8,128)(2,1)} %gather_fusion) | data formatting | bytes 7864320 | tf_op jit(solution)/shard_map/reshape | solution.py:78
  45.5 26.0 %all-to-all-done = bf16[64,3,2,2560]{3,2,1,0:T(2,128)(2,1)S(1)} async-done(((bf16[64,3,2,2560]{3,2,1,0:T(2,128)(2,1)}), bf16[64,3,2,2560]{3,2,1,0:T(2,128)(2,1)S(1)}, u32[]{:S(2)}, u32[]{:S(2)}) %all-to-all-start) | async-done | bytes 1966112 | tf_op jit(solution)/shard_map/all_to_all | solution.py:132
  71.5 6.4 %all-to-all-start.2 = ((bf16[64,6,2,2560]{3,2,1,0:T(2,128)(2,1)}), bf16[64,6,2,2560]{3,2,1,0:T(2,128)(2,1)}, u32[]{:S(2)}, u32[]{:S(2)}) async-start(bf16[64,6,2,2560]{3,2,1,0:T(2,128)(2,1)} %reshape.388), calls=%async_computation.2 | async-start | bytes 7864320 | tf_op jit(solution)/shard_map/all_to_all | solution.py:148
  80.2 5.7 %fusion.10 = f32[384,768]{1,0:T(8,128)} fusion(bf16[384,2560]{1,0:T(8,128)(2,1)} %reshape.382, bf16[1,2560,768]{2,1,0:T(8,128)(2,1)} %param.21), kind=kOutput, calls=%fused_computation.15 | convolution fusion | flops 1509949440 | bytes 7077888 | tf_op jit(solution)/shard_map/dot_general | solution.py:38
  85.9 9.2 %convolution_convert_fusion.1 = bf16[384,2560]{1,0:T(8,128)(2,1)} fusion(bf16[1,768,2560]{2,1,0:T(8,128)(2,1)} %param.23, bf16[384,2560]{1,0:T(8,128)(2,1)S(1)} %copy-done.2, bf16[1,2560,768]{2,1,0:T(8,128)(2,1)} %param.22, f32[384,768]{1,0:T(8,128)} %fusion.10), kind=kOutput, calls=%fused_computation.5 | convolution fusion | flops 3022651392 | bytes 12976128 | tf_op jit(solution)/shard_map/dot_general | solution.py:41
  95.1 5.0 %reshape.383 = bf16[64,3,2,2560]{3,2,1,0:T(2,128)(2,1)} reshape(bf16[384,2560]{1,0:T(8,128)(2,1)} %convolution_convert_fusion.1) | data formatting | bytes 3932160 | tf_op jit(solution)/shard_map/reshape | solution.py:141
  100.1 66.6 %all-to-all-done.2 = bf16[64,6,2,2560]{3,2,1,0:T(2,128)(2,1)} async-done(((bf16[64,6,2,2560]{3,2,1,0:T(2,128)(2,1)}), bf16[64,6,2,2560]{3,2,1,0:T(2,128)(2,1)}, u32[]{:S(2)}, u32[]{:S(2)}) %all-to-all-start.2) | async-done | bytes 3932192 | tf_op jit(solution)/shard_map/all_to_all | solution.py:148
  166.7 5.7 %all-to-all-start.1 = ((bf16[64,3,2,2560]{3,2,1,0:T(2,128)(2,1)}), bf16[64,3,2,2560]{3,2,1,0:T(2,128)(2,1)S(1)}, u32[]{:S(2)}, u32[]{:S(2)}) async-start(bf16[64,3,2,2560]{3,2,1,0:T(2,128)(2,1)} %reshape.383), calls=%async_computation.1 | async-start | bytes 3932160 | tf_op jit(solution)/shard_map/all_to_all | solution.py:140
  172.4 9.1 %reshape.389 = bf16[768,2560]{1,0:T(8,128)(2,1)} reshape(bf16[64,6,2,2560]{3,2,1,0:T(2,128)(2,1)} %all-to-all-done.2) | data formatting | bytes 7864320 | tf_op jit(solution)/shard_map/reshape | solution.py:155
  181.4 6.6 %fusion.4 = f32[768,768]{1,0:T(8,128)S(1)} fusion(bf16[768,2560]{1,0:T(8,128)(2,1)} %reshape.389, bf16[1,2560,768]{2,1,0:T(8,128)(2,1)} %param.22), kind=kOutput, calls=%fused_computation.9 | convolution fusion | flops 3019898880 | bytes 10223616 | tf_op jit(solution)/shard_map/dot_general | solution.py:39
  188.1 3.4 %multiply_convert_fusion = bf16[768,768]{1,0:T(8,128)(2,1)S(1)} fusion(f32[768,768]{1,0:T(8,128)S(1)} %fusion.4, bf16[768,2560]{1,0:T(8,128)(2,1)S(1)} %copy-done, bf16[1,2560,768]{2,1,0:T(8,128)(2,1)S(1)} %copy-done.10), kind=kOutput, calls=%fused_computation.29 | convolution fusion | flops 3023437824 | bytes 11403264 | tf_op jit(solution)/shard_map/dot_general | solution.py:38
  191.6 4.8 %convolution_convert_fusion = bf16[768,2560]{1,0:T(8,128)(2,1)} fusion(bf16[768,768]{1,0:T(8,128)(2,1)S(1)} %multiply_convert_fusion, bf16[1,768,2560]{2,1,0:T(8,128)(2,1)S(1)} %copy-done.11), kind=kOutput, calls=%fused_computation.4 | convolution fusion | flops 3021864960 | bytes 9043968 | tf_op jit(solution)/shard_map/dot_general | solution.py:41
  196.4 8.7 %reshape.390 = bf16[64,6,2,2560]{3,2,1,0:T(2,128)(2,1)} reshape(bf16[768,2560]{1,0:T(8,128)(2,1)} %convolution_convert_fusion) | data formatting | bytes 7864320 | tf_op jit(solution)/shard_map/reshape | solution.py:155
  205.1 13.9 %all-to-all-done.1 = bf16[64,3,2,2560]{3,2,1,0:T(2,128)(2,1)S(1)} async-done(((bf16[64,3,2,2560]{3,2,1,0:T(2,128)(2,1)}), bf16[64,3,2,2560]{3,2,1,0:T(2,128)(2,1)S(1)}, u32[]{:S(2)}, u32[]{:S(2)}) %all-to-all-start.1) | async-done | bytes 1966112 | tf_op jit(solution)/shard_map/all_to_all | solution.py:140
  218.9 6.5 %all-to-all-start.3 = ((bf16[64,6,2,2560]{3,2,1,0:T(2,128)(2,1)}), bf16[64,6,2,2560]{3,2,1,0:T(2,128)(2,1)}, u32[]{:S(2)}, u32[]{:S(2)}) async-start(bf16[64,6,2,2560]{3,2,1,0:T(2,128)(2,1)} %reshape.390), calls=%async_computation.3 | async-start | bytes 7864320 | tf_op jit(solution)/shard_map/all_to_all | solution.py:158
  225.4 2.5 copy.91
  232.5 2.4 fusion.21
  234.9 79.2 %all-to-all-done.3 = bf16[64,6,2,2560]{3,2,1,0:T(2,128)(2,1)} async-done(((bf16[64,6,2,2560]{3,2,1,0:T(2,128)(2,1)}), bf16[64,6,2,2560]{3,2,1,0:T(2,128)(2,1)}, u32[]{:S(2)}, u32[]{:S(2)}) %all-to-all-start.3) | async-done | bytes 3932192 | tf_op jit(solution)/shard_map/all_to_all | solution.py:158
  314.1 3.0 convolution_bitcast_fusion.1
  317.1 3.0 fusion.22
  (96 shorter events, 21.2 us)
Async XLA Ops:
  0.0 2.5 copy-start.9
  0.0 3.8 %copy-start.7 = (s32[2,64,6]{1,0,2:T(2,128)S(1)}, s32[2,64,6]{1,0,2:T(2,128)}, u32[]{:S(2)}) copy-start(s32[2,64,6]{1,0,2:T(2,128)} %param.16) | copy-start | bytes 9220
  1.1 3.1 copy-start.12
  1.2 3.2 copy-start.13
  1.2 3.3 %copy-start.8 = (f32[2,64,6]{1,0,2:T(2,128)S(1)}, f32[2,64,6]{1,0,2:T(2,128)}, u32[]{:S(2)}) copy-start(f32[2,64,6]{1,0,2:T(2,128)} %param.17) | copy-start | bytes 9220
  1.2 4.6 %copy-start.5 = (bf16[2,64,512]{2,1,0:T(8,128)(2,1)S(1)}, bf16[2,64,512]{2,1,0:T(8,128)(2,1)}, u32[]{:S(2)}) copy-start(bf16[2,64,512]{2,1,0:T(8,128)(2,1)} %param.14) | copy-start | bytes 393220
  3.8 2.5 copy-start.6
  6.3 0.8 copy-start.1
  11.5 60.1 %all-to-all-start = ((bf16[64,3,2,2560]{3,2,1,0:T(2,128)(2,1)}), bf16[64,3,2,2560]{3,2,1,0:T(2,128)(2,1)S(1)}, u32[]{:S(2)}, u32[]{:S(2)}) async-start(bf16[64,3,2,2560]{3,2,1,0:T(2,128)(2,1)} %copy.98), calls=%async_computation | async-start | bytes 3932160 | tf_op jit(solution)/shard_map/all_to_all | solution.py:132
  71.5 95.2 %all-to-all-start.2 = ((bf16[64,6,2,2560]{3,2,1,0:T(2,128)(2,1)}), bf16[64,6,2,2560]{3,2,1,0:T(2,128)(2,1)}, u32[]{:S(2)}, u32[]{:S(2)}) async-start(bf16[64,6,2,2560]{3,2,1,0:T(2,128)(2,1)} %reshape.388), calls=%async_computation.2 | async-start | bytes 7864320 | tf_op jit(solution)/shard_map/all_to_all | solution.py:148
  80.2 5.7 %copy-start.2 = (bf16[384,2560]{1,0:T(8,128)(2,1)S(1)}, bf16[384,2560]{1,0:T(8,128)(2,1)}, u32[]{:S(2)}) copy-start(bf16[384,2560]{1,0:T(8,128)(2,1)} %reshape.382) | copy-start | bytes 5898244
  166.7 52.2 %all-to-all-start.1 = ((bf16[64,3,2,2560]{3,2,1,0:T(2,128)(2,1)}), bf16[64,3,2,2560]{3,2,1,0:T(2,128)(2,1)S(1)}, u32[]{:S(2)}, u32[]{:S(2)}) async-start(bf16[64,3,2,2560]{3,2,1,0:T(2,128)(2,1)} %reshape.383), calls=%async_computation.1 | async-start | bytes 3932160 | tf_op jit(solution)/shard_map/all_to_all | solution.py:140
  181.4 6.7 %copy-start = (bf16[768,2560]{1,0:T(8,128)(2,1)S(1)}, bf16[768,2560]{1,0:T(8,128)(2,1)}, u32[]{:S(2)}) copy-start(bf16[768,2560]{1,0:T(8,128)(2,1)} %reshape.389) | copy-start | bytes 11796484
  181.4 6.7 %copy-start.10 = (bf16[1,2560,768]{2,1,0:T(8,128)(2,1)S(1)}, bf16[1,2560,768]{2,1,0:T(8,128)(2,1)}, u32[]{:S(2)}) copy-start(bf16[1,2560,768]{2,1,0:T(8,128)(2,1)} %param.21) | copy-start | bytes 11796484
  188.1 3.5 %copy-start.11 = (bf16[1,768,2560]{2,1,0:T(8,128)(2,1)S(1)}, bf16[1,768,2560]{2,1,0:T(8,128)(2,1)}, u32[]{:S(2)}) copy-start(bf16[1,768,2560]{2,1,0:T(8,128)(2,1)} %param.23) | copy-start | bytes 11796484
  218.9 95.2 %all-to-all-start.3 = ((bf16[64,6,2,2560]{3,2,1,0:T(2,128)(2,1)}), bf16[64,6,2,2560]{3,2,1,0:T(2,128)(2,1)}, u32[]{:S(2)}, u32[]{:S(2)}) async-start(bf16[64,6,2,2560]{3,2,1,0:T(2,128)(2,1)} %reshape.390), calls=%async_computation.3 | async-start | bytes 7864320 | tf_op jit(solution)/shard_map/all_to_all | solution.py:158
  232.5 81.6 %copy-start.4 = (bf16[64,64,6,2]{0,3,2,1:T(2,128)(2,1)S(1)}, bf16[64,64,6,2]{0,3,2,1:T(2,128)(2,1)}, u32[]{:S(2)}) copy-start(bf16[64,64,6,2]{0,3,2,1:T(2,128)(2,1)} %get-tuple-element.17) | copy-start | bytes 294916
  314.1 3.0 copy-start.3

commit v6 on v0

--- a/solution.py
+++ b/solution.py
@@ -78,7 +78,7 @@
     return (padded[source_row].reshape(shape + (normed.shape[1],)), spot)
 
 
-def combine(attn, returned, spot, kept, gates):
+def combine(attn, returned, spot, kept, gates, precision=lax.Precision.HIGHEST):
     slots = returned.size // returned.shape[-1]
     weight = jnp.where(kept, gates, 0.0)
     onehot = (spot[:, :, None] == lax.iota(jnp.int32, slots)[None, None, :]).astype(jnp.float32)
@@ -87,7 +87,7 @@
         "tabc,abcf->tf",
         spread,
         returned.astype(jnp.float32),
-        precision=lax.Precision.HIGHEST,
+        precision=precision,
         preferred_element_type=jnp.float32,
     )
     return (attn + mixed).astype(jnp.bfloat16)
@@ -147,7 +147,7 @@
         received.shape
     )
     back_two = lax.all_to_all(result, "expert", split_axis=0, concat_axis=0, tiled=True)
-    out_two = combine(attn_two, back_two, spot_two, kept_two, gates[1])
+    out_two = combine(attn_two, back_two, spot_two, kept_two, gates[1], lax.Precision.HIGH)
     return jnp.stack([out_one, out_two])
 
 

time: 320 us -> 320 us (level)
  no operation moved by 1% of the time
where the time goes in v6:
time: 320 us; the launch traced here: 318 us
  waiting for transfers between devices  187 us (58%)
  local copies, waits for them, and re-layouts  57.7 us (18%)
  matrix products  39.1 us (12%)
  starting transfers between devices  30.5 us (10%)
  other arithmetic  3.9 us (1%)
    all_to_all x1, waiting for transfers between devices, shards(): lax.all_to_all(result, 'expert', split_axis=0, concat_axis=0, tiled=True)  80.2 us
    all_to_all x1, waiting for transfers between devices, shards(): lax.all_to_all(packed_two, 'expert', split_axis=0, concat_axis=0, tiled=T...  66.6 us
    all_to_all x1, waiting for transfers between devices, shards(): lax.all_to_all(packed_one, 'expert', split_axis=0, concat_axis=0, tiled=T...  26 us
    dot_general x2, matrix products, expert_rows(): jnp.dot(hidden, down_mat, preferred_element_type=jnp.float32)  14 us
    all_to_all x1, waiting for transfers between devices, shards(): lax.all_to_all(result.reshape(received.shape), 'expert', split_axis=0, co...  13.9 us
    all_to_all x1, starting transfers between devices, shards(): lax.all_to_all(packed_one, 'expert', split_axis=0, concat_axis=0, tiled=T...  12 us
    reshape x2, local copies, waits for them, and re-layouts, shards(): received.reshape(-1, features)  11.3 us
    dot_general x2, matrix products, expert_rows(): gate_val = jnp.dot(rows, gate_mat, preferred_element_type=jnp.float32)  9.09 us
  transfers between devices with their start and end apart: 4, of which 4 were waited for; matrix products, arithmetic and copies ran while one was open for 27% of the time, Pallas kernels for 0%

profile of v6, /device:TPU:8, one launch (start us, length us, event | category | flops | bytes accessed | tf_op | source)
XLA Modules:
  0.0 318.4 jit_solution(10682950272127577214)
XLA Ops:
  7.8 3.3 %copy.95 = bf16[64,3,2,2560]{3,2,1,0:T(2,128)(2,1)} copy(bf16[64,3,2,2560]{3,0,2,1:T(8,128)(2,1)S(1)} %convolution_convert_fusion.2) | data formatting | bytes 3932160 | tf_op jit(solution)/shard_map/convert_element_type | solution.py:68
  11.1 12.0 %all-to-all-start = ((bf16[64,3,2,2560]{3,2,1,0:T(2,128)(2,1)}), bf16[64,3,2,2560]{3,2,1,0:T(2,128)(2,1)S(1)}, u32[]{:S(2)}, u32[]{:S(2)}) async-start(bf16[64,3,2,2560]{3,2,1,0:T(2,128)(2,1)} %copy.95), calls=%async_computation | async-start | bytes 3932160 | tf_op jit(solution)/shard_map/all_to_all | solution.py:123
  28.7 3.1 scatter_custom_fusion
  31.8 4.6 %gather_fusion = bf16[768,2560]{1,0:T(8,128)(2,1)} fusion(bf16[65,2560]{1,0:T(8,128)(2,1)S(1)} %concatenate.3, s32[1024]{0:T(1024)S(1)} %pad_clamp_fusion), kind=kCustom, calls=%fused_computation | custom fusion | bytes 7867392 | tf_op jit(solution)/shard_map/gather | solution.py:78
  36.4 8.7 %reshape.388 = bf16[64,6,2,2560]{3,2,1,0:T(2,128)(2,1)} reshape(bf16[768,2560]{1,0:T(8,128)(2,1)} %gather_fusion) | data formatting | bytes 7864320 | tf_op jit(solution)/shard_map/reshape | solution.py:78
  45.1 26.0 %all-to-all-done = bf16[64,3,2,2560]{3,2,1,0:T(2,128)(2,1)S(1)} async-done(((bf16[64,3,2,2560]{3,2,1,0:T(2,128)(2,1)}), bf16[64,3,2,2560]{3,2,1,0:T(2,128)(2,1)S(1)}, u32[]{:S(2)}, u32[]{:S(2)}) %all-to-all-start) | async-done | bytes 1966112 | tf_op jit(solution)/shard_map/all_to_all | solution.py:123
  71.1 6.4 %all-to-all-start.2 = ((bf16[64,6,2,2560]{3,2,1,0:T(2,128)(2,1)}), bf16[64,6,2,2560]{3,2,1,0:T(2,128)(2,1)}, u32[]{:S(2)}, u32[]{:S(2)}) async-start(bf16[64,6,2,2560]{3,2,1,0:T(2,128)(2,1)} %reshape.388), calls=%async_computation.2 | async-start | bytes 7864320 | tf_op jit(solution)/shard_map/all_to_all | solution.py:139
  77.6 2.3 reshape.382
  79.9 5.7 %fusion.10 = f32[384,768]{1,0:T(8,128)} fusion(bf16[384,2560]{1,0:T(8,128)(2,1)} %reshape.382, bf16[1,2560,768]{2,1,0:T(8,128)(2,1)} %param.21), kind=kOutput, calls=%fused_computation.15 | convolution fusion | flops 1509949440 | bytes 7077888 | tf_op jit(solution)/shard_map/dot_general | solution.py:38
  85.5 9.2 %convolution_convert_fusion.1 = bf16[384,2560]{1,0:T(8,128)(2,1)} fusion(bf16[1,768,2560]{2,1,0:T(8,128)(2,1)} %param.23, bf16[384,2560]{1,0:T(8,128)(2,1)S(1)} %copy-done.2, bf16[1,2560,768]{2,1,0:T(8,128)(2,1)} %param.22, f32[384,768]{1,0:T(8,128)} %fusion.10), kind=kOutput, calls=%fused_computation.5 | convolution fusion | flops 3022651392 | bytes 12976128 | tf_op jit(solution)/shard_map/dot_general | solution.py:41
  94.7 5.0 %reshape.383 = bf16[64,3,2,2560]{3,2,1,0:T(2,128)(2,1)} reshape(bf16[384,2560]{1,0:T(8,128)(2,1)} %convolution_convert_fusion.1) | data formatting | bytes 3932160 | tf_op jit(solution)/shard_map/reshape | solution.py:132
  99.7 66.6 %all-to-all-done.2 = bf16[64,6,2,2560]{3,2,1,0:T(2,128)(2,1)} async-done(((bf16[64,6,2,2560]{3,2,1,0:T(2,128)(2,1)}), bf16[64,6,2,2560]{3,2,1,0:T(2,128)(2,1)}, u32[]{:S(2)}, u32[]{:S(2)}) %all-to-all-start.2) | async-done | bytes 3932192 | tf_op jit(solution)/shard_map/all_to_all | solution.py:139
  166.3 5.7 %all-to-all-start.1 = ((bf16[64,3,2,2560]{3,2,1,0:T(2,128)(2,1)}), bf16[64,3,2,2560]{3,2,1,0:T(2,128)(2,1)S(1)}, u32[]{:S(2)}, u32[]{:S(2)}) async-start(bf16[64,3,2,2560]{3,2,1,0:T(2,128)(2,1)} %reshape.383), calls=%async_computation.1 | async-start | bytes 3932160 | tf_op jit(solution)/shard_map/all_to_all | solution.py:131
  172.0 9.1 %reshape.389 = bf16[768,2560]{1,0:T(8,128)(2,1)} reshape(bf16[64,6,2,2560]{3,2,1,0:T(2,128)(2,1)} %all-to-all-done.2) | data formatting | bytes 7864320 | tf_op jit(solution)/shard_map/reshape | solution.py:146
  181.1 6.6 %fusion.4 = f32[768,768]{1,0:T(8,128)S(1)} fusion(bf16[768,2560]{1,0:T(8,128)(2,1)} %reshape.389, bf16[1,2560,768]{2,1,0:T(8,128)(2,1)} %param.22), kind=kOutput, calls=%fused_computation.9 | convolution fusion | flops 3019898880 | bytes 10223616 | tf_op jit(solution)/shard_map/dot_general | solution.py:39
  187.8 3.4 %multiply_convert_fusion = bf16[768,768]{1,0:T(8,128)(2,1)S(1)} fusion(f32[768,768]{1,0:T(8,128)S(1)} %fusion.4, bf16[768,2560]{1,0:T(8,128)(2,1)S(1)} %copy-done, bf16[1,2560,768]{2,1,0:T(8,128)(2,1)S(1)} %copy-done.8), kind=kOutput, calls=%fused_computation.27 | convolution fusion | flops 3023437824 | bytes 11403264 | tf_op jit(solution)/shard_map/dot_general | solution.py:38
  191.2 4.8 %convolution_convert_fusion = bf16[768,2560]{1,0:T(8,128)(2,1)} fusion(bf16[768,768]{1,0:T(8,128)(2,1)S(1)} %multiply_convert_fusion, bf16[1,768,2560]{2,1,0:T(8,128)(2,1)S(1)} %copy-done.9), kind=kOutput, calls=%fused_computation.4 | convolution fusion | flops 3021864960 | bytes 9043968 | tf_op jit(solution)/shard_map/dot_general | solution.py:41
  196.0 8.7 %reshape.390 = bf16[64,6,2,2560]{3,2,1,0:T(2,128)(2,1)} reshape(bf16[768,2560]{1,0:T(8,128)(2,1)} %convolution_convert_fusion) | data formatting | bytes 7864320 | tf_op jit(solution)/shard_map/reshape | solution.py:146
  204.7 13.9 %all-to-all-done.1 = bf16[64,3,2,2560]{3,2,1,0:T(2,128)(2,1)S(1)} async-done(((bf16[64,3,2,2560]{3,2,1,0:T(2,128)(2,1)}), bf16[64,3,2,2560]{3,2,1,0:T(2,128)(2,1)S(1)}, u32[]{:S(2)}, u32[]{:S(2)}) %all-to-all-start.1) | async-done | bytes 1966112 | tf_op jit(solution)/shard_map/all_to_all | solution.py:131
  218.6 6.4 %all-to-all-start.3 = ((bf16[64,6,2,2560]{3,2,1,0:T(2,128)(2,1)}), bf16[64,6,2,2560]{3,2,1,0:T(2,128)(2,1)}, u32[]{:S(2)}, u32[]{:S(2)}) async-start(bf16[64,6,2,2560]{3,2,1,0:T(2,128)(2,1)} %reshape.390), calls=%async_computation.3 | async-start | bytes 7864320 | tf_op jit(solution)/shard_map/all_to_all | solution.py:149
  225.0 2.6 copy.88
  231.2 2.4 fusion.25
  233.6 80.2 %all-to-all-done.3 = bf16[64,6,2,2560]{3,2,1,0:T(2,128)(2,1)} async-done(((bf16[64,6,2,2560]{3,2,1,0:T(2,128)(2,1)}), bf16[64,6,2,2560]{3,2,1,0:T(2,128)(2,1)}, u32[]{:S(2)}, u32[]{:S(2)}) %all-to-all-start.3) | async-done | bytes 3932192 | tf_op jit(solution)/shard_map/all_to_all | solution.py:149
  313.8 3.8 %fusion.26 = bf16[1,64,2560]{2,1,0:T(8,128)(2,1)S(1)} fusion(f32[64,2560]{1,0:T(8,128)S(1)} %reshape.386, bf16[64,6,2,2560]{3,2,1,0:T(2,128)(2,1)} %all-to-all-done.3, f32[64,64,6,2]{0,3,2,1:T(2,128)S(1)} %bitcast.123), kind=kOutput, calls=%fused_computation.26 | convolution fusion | flops 755302400 | bytes 5111808 | tf_op jit(solution)/shard_map/tabc,abcf->tf/dot_general | solution.py:86
  (90 shorter events, 17.5 us)
Async XLA Ops:
  0.0 2.5 copy-start.7
  0.0 3.8 %copy-start.5 = (s32[2,64,6]{1,0,2:T(2,128)S(1)}, s32[2,64,6]{1,0,2:T(2,128)}, u32[]{:S(2)}) copy-start(s32[2,64,6]{1,0,2:T(2,128)} %param.16) | copy-start | bytes 9220
  1.1 3.1 copy-start.10
  1.2 3.2 %copy-start.11 = (s32[64]{0:T(128)S(1)}, s32[64]{0:T(128)}, u32[]{:S(2)}) copy-start(s32[64]{0:T(128)} %param.19) | copy-start | bytes 772
  1.2 3.3 %copy-start.6 = (f32[2,64,6]{1,0,2:T(2,128)S(1)}, f32[2,64,6]{1,0,2:T(2,128)}, u32[]{:S(2)}) copy-start(f32[2,64,6]{1,0,2:T(2,128)} %param.17) | copy-start | bytes 9220
  1.2 4.6 %copy-start.3 = (bf16[2,64,512]{2,1,0:T(8,128)(2,1)S(1)}, bf16[2,64,512]{2,1,0:T(8,128)(2,1)}, u32[]{:S(2)}) copy-start(bf16[2,64,512]{2,1,0:T(8,128)(2,1)} %param.14) | copy-start | bytes 393220
  3.8 2.5 copy-start.4
  6.3 1.5 copy-start.1
  11.1 60.1 %all-to-all-start = ((bf16[64,3,2,2560]{3,2,1,0:T(2,128)(2,1)}), bf16[64,3,2,2560]{3,2,1,0:T(2,128)(2,1)S(1)}, u32[]{:S(2)}, u32[]{:S(2)}) async-start(bf16[64,3,2,2560]{3,2,1,0:T(2,128)(2,1)} %copy.95), calls=%async_computation | async-start | bytes 3932160 | tf_op jit(solution)/shard_map/all_to_all | solution.py:123
  71.1 95.2 %all-to-all-start.2 = ((bf16[64,6,2,2560]{3,2,1,0:T(2,128)(2,1)}), bf16[64,6,2,2560]{3,2,1,0:T(2,128)(2,1)}, u32[]{:S(2)}, u32[]{:S(2)}) async-start(bf16[64,6,2,2560]{3,2,1,0:T(2,128)(2,1)} %reshape.388), calls=%async_computation.2 | async-start | bytes 7864320 | tf_op jit(solution)/shard_map/all_to_all | solution.py:139
  79.9 5.7 %copy-start.2 = (bf16[384,2560]{1,0:T(8,128)(2,1)S(1)}, bf16[384,2560]{1,0:T(8,128)(2,1)}, u32[]{:S(2)}) copy-start(bf16[384,2560]{1,0:T(8,128)(2,1)} %reshape.382) | copy-start | bytes 5898244
  166.3 52.2 %all-to-all-start.1 = ((bf16[64,3,2,2560]{3,2,1,0:T(2,128)(2,1)}), bf16[64,3,2,2560]{3,2,1,0:T(2,128)(2,1)S(1)}, u32[]{:S(2)}, u32[]{:S(2)}) async-start(bf16[64,3,2,2560]{3,2,1,0:T(2,128)(2,1)} %reshape.383), calls=%async_computation.1 | async-start | bytes 3932160 | tf_op jit(solution)/shard_map/all_to_all | solution.py:131
  181.1 6.7 %copy-start = (bf16[768,2560]{1,0:T(8,128)(2,1)S(1)}, bf16[768,2560]{1,0:T(8,128)(2,1)}, u32[]{:S(2)}) copy-start(bf16[768,2560]{1,0:T(8,128)(2,1)} %reshape.389) | copy-start | bytes 11796484
  181.1 6.7 %copy-start.8 = (bf16[1,2560,768]{2,1,0:T(8,128)(2,1)S(1)}, bf16[1,2560,768]{2,1,0:T(8,128)(2,1)}, u32[]{:S(2)}) copy-start(bf16[1,2560,768]{2,1,0:T(8,128)(2,1)} %param.21) | copy-start | bytes 11796484
  187.7 3.5 %copy-start.9 = (bf16[1,768,2560]{2,1,0:T(8,128)(2,1)S(1)}, bf16[1,768,2560]{2,1,0:T(8,128)(2,1)}, u32[]{:S(2)}) copy-start(bf16[1,768,2560]{2,1,0:T(8,128)(2,1)} %param.23) | copy-start | bytes 11796484
  218.6 95.2 %all-to-all-start.3 = ((bf16[64,6,2,2560]{3,2,1,0:T(2,128)(2,1)}), bf16[64,6,2,2560]{3,2,1,0:T(2,128)(2,1)}, u32[]{:S(2)}, u32[]{:S(2)}) async-start(bf16[64,6,2,2560]{3,2,1,0:T(2,128)(2,1)} %reshape.390), calls=%async_computation.3 | async-start | bytes 7864320 | tf_op jit(solution)/shard_map/all_to_all | solution.py:149
